TPU v7x, 32 devices: a whole 2x2x4 slice. The times are simulated.
32 devices in a mesh: wide: 16 (over z, y, x), lev: 2 (over core).
Axes of the slice: x: 2, y: 2, z: 4, core: 2. Of those that a mesh axis runs over, the one named last changes fastest.
Arguments:
- alpha: bfloat16 [16, 4, 64, 1024], P('wide', None, 'lev'), may hold values from -6 to 6
- ens: bfloat16 [16, 4, 64, 1024], P('wide', None, 'lev'), may hold values from -6 to 6
- htile: bfloat16 [8, 128, 128], replicated, may hold values from -0.1875 to 0.1875
- vloc: float32 [64, 9], replicated, may hold values from 0.1 to 0.55
- pattern: int32 [8, 8], replicated, may hold values from 0 to 7
- region_sizes: int32 [16], replicated, may hold values from 1 to 128, 1024 in all
- owner: int32 [16], replicated, may hold values from 0 to 15, each once
- cotangent: bfloat16 [4, 64, 2048], P(None, 'lev', 'wide'), may hold values from -6 to 6
Outputs:
- increment: bfloat16 [4, 64, 2048], P(None, 'lev', 'wide')
- gradient: bfloat16 [16, 4, 64, 1024], P('wide', None, 'lev')
Inputs may be any that keep to these rules, and one draw needn't show every extreme that they name: `region_sizes`: the entries sum to 1024; the largest equals 128. `owner`: each index of wide appears once. `pattern`: entries of a row may repeat.
All inputs are finite; a program needn't handle non-finite values.
Results may differ from a plain program's by a relative error of at most 0.008.
Values may be sent and summed in bfloat16 or wider, within the bound.
No kernel may reach another device: no remote copies, remote signals or barrier semaphores. Data moves between devices by JAX's collectives and lax.ppermute only.
A program may use at most 128 MiB of HBM per device.

v0:
```python
import math

import jax
import jax.numpy as jnp
from jax import lax
from jax.sharding import PartitionSpec as P

VREACH = 4


def padded_2(block, sides, width):
    for axis, dim in sides:
        count = lax.axis_size(axis)
        forward = [(i, i + 1) for i in range(count - 1)]
        backward = [(target, source) for source, target in forward]
        low = lax.ppermute(
            lax.slice_in_dim(block, block.shape[dim] - width, None, axis=dim), axis, forward
        )
        high = lax.ppermute(lax.slice_in_dim(block, 0, width, axis=dim), axis, backward)
        block = jnp.concatenate([low, block, high], axis=dim)
    return block


def slot_tables(region_sizes, owner, columns, region_max):
    region_ends = jnp.cumsum(region_sizes)
    region_starts = region_ends - region_sizes
    column_ids = jnp.arange(columns, dtype=jnp.int32)
    region_of = jnp.sum((region_ends[None, :] <= column_ids[:, None]).astype(jnp.int32), axis=1)
    slot_of = owner[region_of] * region_max + column_ids - region_starts[region_of]
    holder = jnp.argsort(owner)
    offsets = jnp.arange(region_max, dtype=jnp.int32)
    source = region_starts[holder][:, None] + offsets[None, :]
    valid_slot = offsets[None, :] < region_sizes[holder][:, None]
    source = jnp.where(valid_slot, source, 0).reshape(-1)
    return (slot_of, source, valid_slot.reshape(-1))


def spread_blocks(values, pattern, htile):
    slots = htile.shape[0]
    tile_width = htile.shape[1]
    blocks = values.shape[3] // tile_width
    flat_rows = values.reshape(-1, blocks, tile_width)
    block_ids = jnp.arange(blocks, dtype=jnp.int32)
    selected = []
    for k in range(slots):
        selector = (block_ids[:, None] == pattern[:, k][None, :]).astype(jnp.bfloat16)
        picked = jnp.einsum("rbi,bc->rci", flat_rows, selector, preferred_element_type=jnp.float32)
        selected.append(picked.astype(jnp.bfloat16))
    stacked = jnp.concatenate(selected, axis=2)
    stacked_tiles = htile.reshape(slots * tile_width, tile_width)
    summed = jnp.einsum("rck,kj->rcj", stacked, stacked_tiles, preferred_element_type=jnp.float32)
    return summed.reshape(values.shape).astype(jnp.bfloat16)


def gather_blocks(values, pattern, htile):
    slots = htile.shape[0]
    tile_width = htile.shape[1]
    blocks = values.shape[3] // tile_width
    flat_rows = values.reshape(-1, blocks, tile_width)
    block_ids = jnp.arange(blocks, dtype=jnp.int32)
    selected = []
    for k in range(slots):
        selector = (pattern[:, k][:, None] == block_ids[None, :]).astype(jnp.bfloat16)
        picked = jnp.einsum("rbi,bc->rci", flat_rows, selector, preferred_element_type=jnp.float32)
        selected.append(picked.astype(jnp.bfloat16))
    stacked = jnp.concatenate(selected, axis=2)
    stacked_tiles = jnp.transpose(htile, (0, 2, 1)).reshape(slots * tile_width, tile_width)
    summed = jnp.einsum("rck,kj->rcj", stacked, stacked_tiles, preferred_element_type=jnp.float32)
    return summed.reshape(values.shape).astype(jnp.bfloat16)


def level_window(vloc, levels_here, band_reach):
    first_level = lax.axis_index("lev") * levels_here
    padded = jnp.pad(vloc, ((band_reach, band_reach), (0, 0)))
    return lax.dynamic_slice_in_dim(padded, first_level, levels_here + 2 * band_reach, 0)


def mix_down(extended, window, band_reach, levels_here):
    shape_out = extended.shape[:2] + (levels_here,) + extended.shape[3:]
    summed = jnp.zeros(shape_out, jnp.float32)
    for offset in range(-band_reach, band_reach + 1):
        weight = window[band_reach : band_reach + levels_here, offset + band_reach]
        lower = band_reach + offset
        summed = summed + weight[None, None, :, None] * extended[
            :, :, lower : lower + levels_here
        ].astype(jnp.float32)
    return summed.astype(jnp.bfloat16)


def mix_up(extended, window, band_reach, levels_here):
    shape_out = extended.shape[:2] + (levels_here,) + extended.shape[3:]
    summed = jnp.zeros(shape_out, jnp.float32)
    for offset in range(-band_reach, band_reach + 1):
        lower = band_reach - offset
        weight = window[lower : lower + levels_here, offset + band_reach]
        summed = summed + weight[None, None, :, None] * extended[
            :, :, lower : lower + levels_here
        ].astype(jnp.float32)
    return summed.astype(jnp.bfloat16)


def body(alpha, ens, htile, vloc, pattern, region_sizes, owner, cotangent):
    band_reach = VREACH
    levels_here = alpha.shape[2]
    columns = alpha.shape[3]
    region_max = cotangent.shape[2]
    member_scale = 1.0 / math.sqrt(alpha.shape[0] * lax.axis_size("wide"))
    window = level_window(vloc, levels_here, band_reach)
    slot_of, source, valid_slot = slot_tables(region_sizes, owner, columns, region_max)
    spread_field = spread_blocks(alpha, pattern, htile)
    extended = padded_2(spread_field, (("lev", 2),), band_reach)
    localized = mix_down(extended, window, band_reach, levels_here)
    keep_mask = valid_slot.astype(jnp.bfloat16)
    local_slots = jnp.take(localized, source, axis=3) * keep_mask
    ens_slots = jnp.take(ens, source, axis=3) * keep_mask
    local_here, ens_here = (
        lax.all_to_all(local_slots, "wide", split_axis=3, concat_axis=0, tiled=True),
        lax.all_to_all(ens_slots, "wide", split_axis=3, concat_axis=0, tiled=True),
    )
    products = ens_here.astype(jnp.float32) * local_here.astype(jnp.float32)
    increment = (jnp.sum(products, axis=0) * member_scale).astype(jnp.bfloat16)
    adjoint_here = (ens_here.astype(jnp.float32) * cotangent.astype(jnp.float32)[None]).astype(
        jnp.bfloat16
    )
    returned = lax.all_to_all(adjoint_here, "wide", split_axis=0, concat_axis=3, tiled=True)
    scaled = jnp.take(returned, slot_of, axis=3)
    extended_back = padded_2(scaled, (("lev", 2),), band_reach)
    adjoint_mix = mix_up(extended_back, window, band_reach, levels_here)
    gradient = gather_blocks(adjoint_mix, pattern, htile)
    return (increment, gradient)


def solution(mesh):
    placed = (
        P("wide", None, "lev", None),
        P("wide", None, "lev", None),
        P(),
        P(),
        P(),
        P(),
        P(),
        P(None, "lev", "wide"),
    )
    return jax.shard_map(
        body,
        mesh=mesh,
        in_specs=placed,
        out_specs=(P(None, "lev", "wide"), P("wide", None, "lev", None)),
        check_vma=False,
    )
```

profile of v0, /device:TPU:0, one launch (start us, length us, event | category | flops | bytes accessed | tf_op | source)
XLA Modules:
  0.0 148.0 jit_solution(13125624961536484533)
XLA Ops:
  0.6 1.3 slice_reduce_fusion
  2.0 1.0 copy.109
  3.0 0.3 fusion.1
  3.3 0.3 fusion.3
  3.6 0.3 fusion.5
  3.9 0.3 fusion.7
  4.2 0.3 fusion.9
  4.5 0.3 fusion.11
  4.8 0.3 fusion.13
  5.1 0.3 fusion.15
  5.5 0.7 convolution_convert_fusion.9
  6.4 1.3 collective-permute-start.1
  7.7 3.0 %collective-permute-start = (bf16[1,4,4,1024]{3,2,1,0:T(4,128)(2,1)S(1)}, bf16[1,4,4,1024]{3,2,1,0:T(4,128)(2,1)S(1)}, u32[]{:S(2)}, u32[]{:S(2)}) collective-permute-start(bf16[1,4,4,1024]{3,2,1,0:T(4,128)(2,1)S(1)} %get-tuple-element.37), channel_id=1, source_target_pairs={{0,1},{2,3},{4,5},{6,7},{8,9},{10,11},{12,13},{14,15},{16,17},{18,... | collective-permute-start | bytes 98312 | tf_op jit(solution)/shard_map/ppermute | solution.py:16
  11.1 0.7 fusion.103
  11.8 0.7 fusion.102
  12.5 4.4 %compare_select_fusion.4 = (s32[1024,1]{0,1:T(1,128)S(1)}, s32[1024,1]{0,1:T(1,128)S(1)}) fusion(s32[]{:T(128)} %bitcast.54, s32[]{:T(128)} %bitcast.55, s32[]{:T(128)} %bitcast.56, s32[]{:T(128)} %bitcast.57, s32[]{:T(128)} %bitcast.58, s32[]{:T(128)} %bitcast.60, s32[]{:T(128)} %bitcast.59, s32[1024,1]{0,1:T(1,128)S(1)} %bitcast.312), kind=kLoop, calls=%fused_computation.115 | loop fusion | flops 15360 | bytes 12316 | tf_op jit(solution)/shard_map/gather | solution.py:29
  17.1 1.2 sort.17
  18.3 4.5 %compare_select_fusion.5 = s32[1024,1]{0,1:T(1,128)S(1)} fusion(s32[1024,1]{0,1:T(1,128)S(1)} %get-tuple-element.32, s32[]{:T(128)} %bitcast.71, s32[]{:T(128)} %bitcast.72, s32[]{:T(128)} %bitcast.73, s32[]{:T(128)} %bitcast.74, s32[]{:T(128)} %bitcast.75, s32[]{:T(128)} %bitcast.77, s32[]{:T(128)} %bitcast.76), kind=kLoop, calls=%fused_computation.116 | loop fusion | flops 12288 | bytes 8220 | tf_op jit(solution)/shard_map/gather | solution.py:29
  22.9 11.8 %compare_and_fusion = (pred[1024]{0:T(1024)(128)(4,1)}, s32[1024]{0:T(1024)S(1)}, s32[1024]{0:T(1024)S(1)}) fusion(pred[1024]{0:T(1024)(128)(4,1)S(1)} %get-tuple-element.19, pred[1024]{0:T(1024)(128)(4,1)S(1)} %get-tuple-element.18, pred[1024]{0:T(1024)(128)(4,1)S(1)} %get-tuple-element.17, pred[1024]{0:T(1024)(128)(4,1)S(1)} %get-tuple-element.16, ...), kind=kLoop, calls=%fused_computation.177 | loop fusion | flops 27648 | bytes 26696 | tf_op jit(solution)/shard_map/jit(_take)/and | solution.py:126
  34.6 0.7 gather_fusion
  35.3 0.7 gather_fusion.1
  36.2 0.7 dynamic-slice_bitcast_fusion.7
  36.9 0.7 dynamic-slice_bitcast_fusion.6
  37.5 1.4 copy.95
  38.9 8.0 %gather_fusion.3 = bf16[2048,4,32]{2,1,0:T(4,128)(2,1)S(1)} fusion(bf16[4,32,1024]{1,0,2:T(4,128)(2,1)} %bitcast.301, s32[2048]{0:T(1024)S(1)} %fusion.46), kind=kCustom, calls=%fused_computation.clone | custom fusion | bytes 1056768 | tf_op jit(solution)/shard_map/jit(_take)/gather | solution.py:115
  47.0 2.2 %copy.96 = bf16[2048,4,32]{0,2,1:T(8,128)(2,1)} copy(bf16[2048,4,32]{2,1,0:T(4,128)(2,1)S(1)} %gather_fusion.3) | data formatting | bytes 1048576 | tf_op jit(solution)/shard_map/jit(_take)/gather | solution.py:115
  49.3 0.7 fusion.45
  50.0 0.7 copy.99
  50.7 6.8 %gather_fusion.4 = bf16[2048,4,32]{2,1,0:T(4,128)(2,1)S(1)} fusion(bf16[4,32,1024]{1,0,2:T(4,128)(2,1)S(1)} %copy.99, s32[2048]{0:T(1024)S(1)} %fusion.46), kind=kCustom, calls=%fused_computation.1.clone | custom fusion | bytes 1056768 | tf_op jit(solution)/shard_map/jit(_take)/gather | solution.py:114
  57.6 1.2 copy.100
  58.7 0.9 fusion.35
  59.6 2.8 %copy.101 = bf16[1,4,32,2048]{2,1,0,3:T(4,128)(2,1)S(1)} copy(bf16[1,4,32,2048]{3,2,1,0:T(8,128)(2,1)} %get-tuple-element.57) | data formatting | bytes 1048576 | tf_op jit(solution)/shard_map/mul | solution.py:114
  62.4 2.7 %reshape.466 = bf16[16,2,8192]{2,1,0:T(2,128)(2,1)} reshape(bf16[2048,1,4,32]{3,2,1,0:T(4,128)(2,1)S(1)} %bitcast.296) | data formatting | bytes 1048576
  65.1 8.3 %all-to-all-start.1 = ((bf16[16,2,8192]{2,1,0:T(2,128)(2,1)}), bf16[16,2,8192]{2,1,0:T(2,128)(2,1)S(1)}, u32[]{:S(2)}, u32[]{:S(2)}) async-start(bf16[16,2,8192]{2,1,0:T(2,128)(2,1)} %reshape.466), calls=%async_computation.1 | async-start | bytes 1048576 | tf_op jit(solution)/shard_map/all_to_all | solution.py:117
  73.4 1.4 copy.97
  74.8 2.7 %reshape.468 = bf16[16,2,8192]{2,1,0:T(2,128)(2,1)} reshape(bf16[2048,1,4,32]{3,2,1,0:T(4,128)(2,1)S(1)} %bitcast.297) | data formatting | bytes 1048576
  77.5 10.6 %all-to-all-done.1 = bf16[16,2,8192]{2,1,0:T(2,128)(2,1)S(1)} async-done(((bf16[16,2,8192]{2,1,0:T(2,128)(2,1)}), bf16[16,2,8192]{2,1,0:T(2,128)(2,1)S(1)}, u32[]{:S(2)}, u32[]{:S(2)}) %all-to-all-start.1) | async-done | bytes 524320 | tf_op jit(solution)/shard_map/all_to_all | solution.py:117
  88.1 4.4 %all-to-all-start = ((bf16[16,2,8192]{2,1,0:T(2,128)(2,1)}), bf16[16,2,8192]{2,1,0:T(2,128)(2,1)}, u32[]{:S(2)}, u32[]{:S(2)}) async-start(bf16[16,2,8192]{2,1,0:T(2,128)(2,1)} %reshape.468), calls=%async_computation | async-start | bytes 1048576 | tf_op jit(solution)/shard_map/all_to_all | solution.py:118
  92.5 3.6 %reshape.467 = bf16[2048,1,4,32]{3,2,1,0:T(4,128)(2,1)S(1)} reshape(bf16[16,2,8192]{2,1,0:T(2,128)(2,1)} %copy-done.2) | data formatting | bytes 1048576
  96.2 0.9 copy.102
  97.1 9.5 %all-to-all-done = bf16[16,2,8192]{2,1,0:T(2,128)(2,1)} async-done(((bf16[16,2,8192]{2,1,0:T(2,128)(2,1)}), bf16[16,2,8192]{2,1,0:T(2,128)(2,1)}, u32[]{:S(2)}, u32[]{:S(2)}) %all-to-all-start) | async-done | bytes 524320 | tf_op jit(solution)/shard_map/all_to_all | solution.py:118
  106.6 3.6 %reshape.469 = bf16[2048,1,4,32]{3,2,1,0:T(4,128)(2,1)S(1)} reshape(bf16[16,2,8192]{2,1,0:T(2,128)(2,1)} %all-to-all-done) | data formatting | bytes 1048576
  110.2 2.1 %copy.98 = f32[1,4,32,16,128]{4,2,1,3,0:T(8,128)} copy(bf16[1,4,32,16,128]{2,1,4,3,0:T(4,128)(2,1)S(1)} %bitcast.299) | data formatting | bytes 1572864 | tf_op jit(solution)/shard_map/convert_element_type | solution.py:120
  112.3 2.3 %fusion.33 = (bf16[16,4,32,128]{3,2,1,0:T(8,128)(2,1)}, f32[4,32,128]{2,1,0:T(8,128)S(1)}) fusion(f32[1,4,32,16,128]{4,2,1,3,0:T(8,128)} %copy.98, f32[4,32,128]{2,1,0:T(8,128)S(1)} %convert_element_type.309, f32[1,4,32,16,128]{4,2,1,3,0:T(8,128)S(1)} %copy.102), kind=kLoop, calls=%fused_computation.58 | loop fusion | flops 1032192 | bytes 2752512 | tf_op jit(solution)/shard_map/convert_element_type | solution.py:122
  114.6 3.8 %all-to-all-start.2 = ((bf16[16,4,32,128]{3,2,1,0:T(8,128)(2,1)}), bf16[16,4,32,128]{3,2,1,0:T(8,128)(2,1)S(1)}, u32[]{:S(2)}, u32[]{:S(2)}) async-start(bf16[16,4,32,128]{3,2,1,0:T(8,128)(2,1)} %get-tuple-element.33), calls=%async_computation.2 | async-start | bytes 1048576 | tf_op jit(solution)/shard_map/all_to_all | solution.py:125
  118.5 0.9 copy.106
  119.4 13.4 %all-to-all-done.2 = bf16[16,4,32,128]{3,2,1,0:T(8,128)(2,1)S(1)} async-done(((bf16[16,4,32,128]{3,2,1,0:T(8,128)(2,1)}), bf16[16,4,32,128]{3,2,1,0:T(8,128)(2,1)S(1)}, u32[]{:S(2)}, u32[]{:S(2)}) %all-to-all-start.2) | async-done | bytes 524320 | tf_op jit(solution)/shard_map/all_to_all | solution.py:125
  132.8 1.3 copy.104
  134.2 3.6 %gather_fusion.2 = bf16[1024,4,32]{2,1,0:T(4,128)(2,1)S(1)} fusion(bf16[4,32,2048]{1,0,2:T(4,128)(2,1)S(1)} %bitcast.300, s32[1024]{0:T(1024)S(1)} %get-tuple-element.91), kind=kCustom, calls=%fused_computation.4 | custom fusion | bytes 528384 | tf_op jit(solution)/shard_map/jit(_take)/gather | solution.py:126
  137.8 0.6 copy.105
  138.5 1.3 collective-permute-start.2
  139.8 3.0 %collective-permute-start.3 = (bf16[1,4,4,1024]{3,2,1,0:T(4,128)(2,1)S(1)}, bf16[1,4,4,1024]{3,2,1,0:T(4,128)(2,1)S(1)}, u32[]{:S(2)}, u32[]{:S(2)}) collective-permute-start(bf16[1,4,4,1024]{3,2,1,0:T(4,128)(2,1)S(1)} %get-tuple-element.36), channel_id=1, source_target_pairs={{0,1},{2,3},{4,5},{6,7},{8,9},{10,11},{12,13},{14,15},{16,17},{18,... | collective-permute-start | bytes 98312 | tf_op jit(solution)/shard_map/ppermute | solution.py:16
  142.8 0.6 multiply_convert_fusion
  143.5 0.2 collective-permute-done.3
  143.7 0.7 add_convert_fusion
  144.8 0.2 fusion.19
  145.0 0.2 fusion.21
  145.2 0.2 fusion.23
  145.5 0.2 fusion.25
  145.7 0.2 fusion.27
  146.0 0.2 fusion.29
  146.2 0.2 fusion.31
  146.4 0.7 convolution_convert_fusion
  147.1 0.8 convert_element_type.338
  (90 shorter events, 1.5 us)
Async XLA Ops:
  1.9 3.2 %copy-start.9 = (s32[8]{0:T(128)}, s32[8]{0:T(128)S(1)}, u32[]{:S(2)}) copy-start(s32[8]{0:T(128)S(1)} %get-tuple-element.27) | copy-start | bytes 100
  1.9 3.2 %copy-start.11 = (s32[8]{0:T(128)}, s32[8]{0:T(128)S(1)}, u32[]{:S(2)}) copy-start(s32[8]{0:T(128)S(1)} %get-tuple-element.21) | copy-start | bytes 100
  1.9 3.2 %copy-start.13 = (s32[8]{0:T(128)}, s32[8]{0:T(128)S(1)}, u32[]{:S(2)}) copy-start(s32[8]{0:T(128)S(1)} %get-tuple-element.22) | copy-start | bytes 100
  1.9 3.2 %copy-start.15 = (s32[8]{0:T(128)}, s32[8]{0:T(128)S(1)}, u32[]{:S(2)}) copy-start(s32[8]{0:T(128)S(1)} %get-tuple-element.23) | copy-start | bytes 100
  1.9 3.2 %copy-start.17 = (s32[8]{0:T(128)}, s32[8]{0:T(128)S(1)}, u32[]{:S(2)}) copy-start(s32[8]{0:T(128)S(1)} %get-tuple-element.24) | copy-start | bytes 100
  2.0 3.2 %copy-start.19 = (s32[8]{0:T(128)}, s32[8]{0:T(128)S(1)}, u32[]{:S(2)}) copy-start(s32[8]{0:T(128)S(1)} %get-tuple-element.25) | copy-start | bytes 100
  2.0 3.2 %copy-start.21 = (s32[8]{0:T(128)}, s32[8]{0:T(128)S(1)}, u32[]{:S(2)}) copy-start(s32[8]{0:T(128)S(1)} %get-tuple-element.26) | copy-start | bytes 100
  3.0 2.5 %copy-start.3 = (bf16[8,128,128]{2,1,0:T(8,128)(2,1)S(1)}, bf16[8,128,128]{2,1,0:T(8,128)(2,1)}, u32[]{:S(2)}) copy-start(bf16[8,128,128]{2,1,0:T(8,128)(2,1)} %param.12) | copy-start | bytes 786436
  5.1 5.6 %copy-start = (s32[16]{0:T(128)S(1)}, s32[16]{0:T(128)}, u32[]{:S(2)}) copy-start(s32[16]{0:T(128)} %param.15) | copy-start | bytes 196
  5.4 5.7 %copy-start.6 = (s32[16]{0:T(128)S(1)}, s32[16]{0:T(128)}, u32[]{:S(2)}) copy-start(s32[16]{0:T(128)} %param.16) | copy-start | bytes 196
  5.5 30.8 %copy-start.7 = (f32[64,9]{0,1:T(8,128)S(1)}, f32[64,9]{0,1:T(8,128)}, u32[]{:S(2)}) copy-start(f32[64,9]{0,1:T(8,128)} %param.13) | copy-start | bytes 6916
  5.5 32.1 %copy-start.5 = (bf16[1,4,32,1024]{3,2,1,0:T(8,128)(2,1)S(1)}, bf16[1,4,32,1024]{3,2,1,0:T(8,128)(2,1)}, u32[]{:S(2)}) copy-start(bf16[1,4,32,1024]{3,2,1,0:T(8,128)(2,1)} %param.11) | copy-start | bytes 786436
  6.4 42.9 %collective-permute-start.1 = (bf16[1,4,4,1024]{3,2,1,0:T(4,128)(2,1)S(1)}, bf16[1,4,4,1024]{3,2,1,0:T(4,128)(2,1)S(1)}, u32[]{:S(2)}, u32[]{:S(2)}) collective-permute-start(bf16[1,4,4,1024]{3,2,1,0:T(4,128)(2,1)S(1)} %get-tuple-element.38), channel_id=1, source_target_pairs={{1,0},{3,2},{5,4},{7,6},{9,8},{11,10},{13,12},{15,14},{17,16},{19,... | collective-permute-start | bytes 98312 | tf_op jit(solution)/shard_map/ppermute | solution.py:19
  7.7 41.6 %collective-permute-start = (bf16[1,4,4,1024]{3,2,1,0:T(4,128)(2,1)S(1)}, bf16[1,4,4,1024]{3,2,1,0:T(4,128)(2,1)S(1)}, u32[]{:S(2)}, u32[]{:S(2)}) collective-permute-start(bf16[1,4,4,1024]{3,2,1,0:T(4,128)(2,1)S(1)} %get-tuple-element.37), channel_id=1, source_target_pairs={{0,1},{2,3},{4,5},{6,7},{8,9},{10,11},{12,13},{14,15},{16,17},{18,... | collective-permute-start | bytes 98312 | tf_op jit(solution)/shard_map/ppermute | solution.py:16
  36.9 12.4 %copy-start.23 = (f32[32]{0:T(128)}, f32[32]{0:T(128)S(1)}, u32[]{:S(2)}) copy-start(f32[32]{0:T(128)S(1)} %get-tuple-element.44) | copy-start | bytes 388
  57.5 1.2 copy-start.1
  65.1 23.0 %all-to-all-start.1 = ((bf16[16,2,8192]{2,1,0:T(2,128)(2,1)}), bf16[16,2,8192]{2,1,0:T(2,128)(2,1)S(1)}, u32[]{:S(2)}, u32[]{:S(2)}) async-start(bf16[16,2,8192]{2,1,0:T(2,128)(2,1)} %reshape.466), calls=%async_computation.1 | async-start | bytes 1048576 | tf_op jit(solution)/shard_map/all_to_all | solution.py:117
  74.8 17.7 %copy-start.8 = (bf16[4,32,128]{2,1,0:T(8,128)(2,1)S(1)}, bf16[4,32,128]{2,1,0:T(8,128)(2,1)}, u32[]{:S(2)}) copy-start(bf16[4,32,128]{2,1,0:T(8,128)(2,1)} %param.17) | copy-start | bytes 98308
  88.1 4.4 %copy-start.2 = (bf16[16,2,8192]{2,1,0:T(2,128)(2,1)}, bf16[16,2,8192]{2,1,0:T(2,128)(2,1)S(1)}, u32[]{:S(2)}) copy-start(bf16[16,2,8192]{2,1,0:T(2,128)(2,1)S(1)} %all-to-all-done.1) | copy-start | bytes 1572868
  88.1 18.5 %all-to-all-start = ((bf16[16,2,8192]{2,1,0:T(2,128)(2,1)}), bf16[16,2,8192]{2,1,0:T(2,128)(2,1)}, u32[]{:S(2)}, u32[]{:S(2)}) async-start(bf16[16,2,8192]{2,1,0:T(2,128)(2,1)} %reshape.468), calls=%async_computation | async-start | bytes 1048576 | tf_op jit(solution)/shard_map/all_to_all | solution.py:118
  114.6 18.2 %all-to-all-start.2 = ((bf16[16,4,32,128]{3,2,1,0:T(8,128)(2,1)}), bf16[16,4,32,128]{3,2,1,0:T(8,128)(2,1)S(1)}, u32[]{:S(2)}, u32[]{:S(2)}) async-start(bf16[16,4,32,128]{3,2,1,0:T(8,128)(2,1)} %get-tuple-element.33), calls=%async_computation.2 | async-start | bytes 1048576 | tf_op jit(solution)/shard_map/all_to_all | solution.py:125
  132.8 5.6 %copy-start.25 = (pred[1024]{0:T(1024)(128)(4,1)S(1)}, pred[1024]{0:T(1024)(128)(4,1)}, u32[]{:S(2)}) copy-start(pred[1024]{0:T(1024)(128)(4,1)} %get-tuple-element.28) | copy-start | bytes 3076
  132.8 10.9 %copy-start.24 = (f32[32]{0:T(128)S(1)}, f32[32]{0:T(128)}, u32[]{:S(2)}) copy-start(f32[32]{0:T(128)} %copy-done.23) | copy-start | bytes 388
  132.8 10.9 %copy-start.26 = (f32[32]{0:T(128)S(1)}, f32[32]{0:T(128)}, u32[]{:S(2)}) copy-start(f32[32]{0:T(128)} %get-tuple-element.39) | copy-start | bytes 388
  132.8 10.9 %copy-start.27 = (f32[32]{0:T(128)S(1)}, f32[32]{0:T(128)}, u32[]{:S(2)}) copy-start(f32[32]{0:T(128)} %get-tuple-element.48) | copy-start | bytes 388
  132.8 10.9 %copy-start.28 = (f32[32]{0:T(128)S(1)}, f32[32]{0:T(128)}, u32[]{:S(2)}) copy-start(f32[32]{0:T(128)} %get-tuple-element.50) | copy-start | bytes 388
  132.8 10.9 %copy-start.29 = (f32[32]{0:T(128)S(1)}, f32[32]{0:T(128)}, u32[]{:S(2)}) copy-start(f32[32]{0:T(128)} %get-tuple-element.51) | copy-start | bytes 388
  132.8 10.9 %copy-start.30 = (f32[32]{0:T(128)S(1)}, f32[32]{0:T(128)}, u32[]{:S(2)}) copy-start(f32[32]{0:T(128)} %get-tuple-element.52) | copy-start | bytes 388
  132.8 10.9 %copy-start.31 = (f32[32]{0:T(128)S(1)}, f32[32]{0:T(128)}, u32[]{:S(2)}) copy-start(f32[32]{0:T(128)} %get-tuple-element.53) | copy-start | bytes 388
  134.2 10.3 %copy-start.22 = (s32[8]{0:T(128)S(1)}, s32[8]{0:T(128)}, u32[]{:S(2)}) copy-start(s32[8]{0:T(128)} %copy-done.21) | copy-start | bytes 100
  134.2 10.6 %copy-start.20 = (s32[8]{0:T(128)S(1)}, s32[8]{0:T(128)}, u32[]{:S(2)}) copy-start(s32[8]{0:T(128)} %copy-done.19) | copy-start | bytes 100
  137.8 7.2 %copy-start.18 = (s32[8]{0:T(128)S(1)}, s32[8]{0:T(128)}, u32[]{:S(2)}) copy-start(s32[8]{0:T(128)} %copy-done.17) | copy-start | bytes 100
  137.8 7.4 %copy-start.16 = (s32[8]{0:T(128)S(1)}, s32[8]{0:T(128)}, u32[]{:S(2)}) copy-start(s32[8]{0:T(128)} %copy-done.15) | copy-start | bytes 100
  138.4 7.1 %copy-start.14 = (s32[8]{0:T(128)S(1)}, s32[8]{0:T(128)}, u32[]{:S(2)}) copy-start(s32[8]{0:T(128)} %copy-done.13) | copy-start | bytes 100
  138.4 7.3 %copy-start.12 = (s32[8]{0:T(128)S(1)}, s32[8]{0:T(128)}, u32[]{:S(2)}) copy-start(s32[8]{0:T(128)} %copy-done.11) | copy-start | bytes 100
  138.5 5.0 %collective-permute-start.2 = (bf16[1,4,4,1024]{3,2,1,0:T(4,128)(2,1)S(1)}, bf16[1,4,4,1024]{3,2,1,0:T(4,128)(2,1)S(1)}, u32[]{:S(2)}, u32[]{:S(2)}) collective-permute-start(bf16[1,4,4,1024]{3,2,1,0:T(4,128)(2,1)S(1)} %get-tuple-element.35), channel_id=1, source_target_pairs={{1,0},{3,2},{5,4},{7,6},{9,8},{11,10},{13,12},{15,14},{17,16},{19,... | collective-permute-start | bytes 98312 | tf_op jit(solution)/shard_map/ppermute | solution.py:19
  139.8 3.9 %collective-permute-start.3 = (bf16[1,4,4,1024]{3,2,1,0:T(4,128)(2,1)S(1)}, bf16[1,4,4,1024]{3,2,1,0:T(4,128)(2,1)S(1)}, u32[]{:S(2)}, u32[]{:S(2)}) collective-permute-start(bf16[1,4,4,1024]{3,2,1,0:T(4,128)(2,1)S(1)} %get-tuple-element.36), channel_id=1, source_target_pairs={{0,1},{2,3},{4,5},{6,7},{8,9},{10,11},{12,13},{14,15},{16,17},{18,... | collective-permute-start | bytes 98312 | tf_op jit(solution)/shard_map/ppermute | solution.py:16
  143.7 2.2 %copy-start.10 = (s32[8]{0:T(128)S(1)}, s32[8]{0:T(128)}, u32[]{:S(2)}) copy-start(s32[8]{0:T(128)} %copy-done.9) | copy-start | bytes 100
  144.5 1.9 %copy-start.4 = (bf16[8,128,128]{1,2,0:T(8,128)(2,1)S(1)}, bf16[8,128,128]{1,2,0:T(8,128)(2,1)}, u32[]{:S(2)}) copy-start(bf16[8,128,128]{1,2,0:T(8,128)(2,1)} %copy.106) | copy-start | bytes 786436
where the time goes:
time: 149 us; the launch traced here: 148 us
  local copies, waits for them, and re-layouts  54.2 us (36%)
  waiting for transfers between devices  33.7 us (23%)
  other arithmetic  27.8 us (19%)
  starting transfers between devices  25.2 us (17%)
  matrix products  5.5 us (4%)
    unnamed x73, local copies, waits for them, and re-layouts  16 us
    all_to_all x1, waiting for transfers between devices, body(): lax.all_to_all(adjoint_here, 'wide', split_axis=0, concat_axis=3, tiled=T...  13.4 us
    and x1, other arithmetic, body(): scaled = jnp.take(returned, slot_of, axis=3)  11.8 us
    all_to_all x1, waiting for transfers between devices, body(): lax.all_to_all(local_slots, 'wide', split_axis=3, concat_axis=0, tiled=True)  10.6 us
    gather x2, local copies, waits for them, and re-layouts, body(): ens_slots = jnp.take(ens, source, axis=3) * keep_mask  10.3 us
    all_to_all x1, waiting for transfers between devices, body(): lax.all_to_all(ens_slots, 'wide', split_axis=3, concat_axis=0, tiled=True)  9.51 us
    all_to_all x1, starting transfers between devices, body(): lax.all_to_all(local_slots, 'wide', split_axis=3, concat_axis=0, tiled=True)  8.34 us
    gather x2, local copies, waits for them, and re-layouts, body(): local_slots = jnp.take(localized, source, axis=3) * keep_mask  8 us
  transfers between devices with their start and end apart: 7, of which 4 were waited for; matrix products, arithmetic and copies ran while one was open for 33% of the time, Pallas kernels for 0%

commit v1 on v0

v1 whole, which is shorter than its diff:
```python
import functools
import math

import jax
import jax.numpy as jnp
from jax import lax
from jax.experimental import pallas as pl
from jax.experimental.pallas import tpu as pltpu
from jax.sharding import PartitionSpec as P

VREACH = 4
SUB = 8
VMEM = pl.BlockSpec(memory_space=pltpu.VMEM)
SMEM = pl.BlockSpec(memory_space=pltpu.SMEM)


def halo_swap(rows_top, rows_bottom, axis):
    count = lax.axis_size(axis)
    if count == 2:
        both = lax.ppermute(
            jnp.stack([rows_top, rows_bottom]), axis, [(0, 1), (1, 0)]
        )
        return both[0], both[1]
    below = lax.ppermute(rows_top, axis, [(i, i + 1) for i in range(count - 1)])
    above = lax.ppermute(rows_bottom, axis, [(i + 1, i) for i in range(count - 1)])
    return below, above


def split_bf16(value):
    high = value.astype(jnp.bfloat16)
    return high, (value - high.astype(jnp.float32)).astype(jnp.bfloat16)


def weight_kernel(fields, slabs, vloc_ref, down_ref, up_ref, padded):
    reach = VREACH
    levels_all = vloc_ref.shape[0]
    levels = levels_all // slabs
    rows = fields * levels
    halo = fields * reach
    slab = lax.axis_index("lev")
    padded[...] = jnp.zeros_like(padded)
    padded[SUB : SUB + levels_all, :] = vloc_ref[...]
    window = padded[pl.ds(pl.multiple_of(slab * levels, SUB), levels + 2 * SUB), :]
    own = jnp.concatenate([window[SUB : SUB + levels]] * fields, axis=0)
    below = jnp.concatenate([window[SUB - reach : SUB]] * fields, axis=0)
    above = jnp.concatenate([window[SUB + levels : SUB + levels + reach]] * fields, axis=0)

    def iota(shape, dim):
        return lax.broadcasted_iota(jnp.int32, shape, dim)

    def band(weights, shift, same):
        total = jnp.zeros(shift.shape, jnp.float32)
        for tap in range(2 * reach + 1):
            column = jnp.broadcast_to(weights[:, tap : tap + 1], shift.shape)
            total = jnp.where((shift == tap - reach) & same, column, total)
        return total

    row, col = iota((rows, rows), 0), iota((rows, rows), 1)
    same = (row // levels) == (col // levels)
    inner = band(own, col - row, same)

    row, col = iota((rows, halo), 0), iota((rows, halo), 1)
    same = (row // levels) == (col // reach)
    level, step = row % levels, col % reach
    low = band(own, step - reach - level, same & (slab > 0))
    high = band(own, levels + step - level, same & (slab < slabs - 1))
    for part, (start, stop) in (
        (inner, (0, rows)),
        (low, (rows, rows + halo)),
        (high, (rows + halo, rows + 2 * halo)),
    ):
        first, second = split_bf16(part)
        down_ref[0, :, start:stop] = first
        down_ref[1, :, start:stop] = second

    row, col = iota((halo, rows), 0), iota((halo, rows), 1)
    same = (row // reach) == (col // levels)
    step, level = row % reach, col % levels
    low = band(below, level - (step - reach), same & (slab > 0))
    high = band(above, level - (levels + step), same & (slab < slabs - 1))
    for part, (start, stop) in (
        (inner, (0, rows)),
        (low, (rows, rows + halo)),
        (high, (rows + halo, rows + 2 * halo)),
    ):
        first, second = split_bf16(part)
        up_ref[0, start:stop, :] = first
        up_ref[1, start:stop, :] = second


def region_loop(sizes_ref, owner_ref, width, body):
    def step(region, start):
        size = sizes_ref[region]
        body(owner_ref[region], start // width, start % width, size)
        return start + size

    lax.fori_loop(0, sizes_ref.shape[0], step, jnp.int32(0), unroll=4)


def forward_kernel(
    inner, pattern_ref, sizes_ref, owner_ref, alpha_ref, halo_ref, down_ref, ens_ref, htile_ref,
    out_ref, mixed, product,
):
    blocks, slots = pattern_ref.shape
    rows = alpha_ref.shape[0]
    width = htile_ref.shape[1]
    span = rows + halo_ref.shape[0]
    extended = jnp.concatenate([alpha_ref[...], halo_ref[...]], axis=0)
    summed = jnp.dot(down_ref[0], extended, preferred_element_type=jnp.float32)
    summed = summed + jnp.dot(down_ref[1], extended, preferred_element_type=jnp.float32)
    for b in range(blocks):
        mixed[b] = summed[:, b * width : (b + 1) * width].astype(jnp.bfloat16)

    def spread(b, carry):
        picked = jnp.concatenate([mixed[pattern_ref[b, k]] for k in range(slots)], axis=1)
        localized = jnp.dot(picked, htile_ref[...], preferred_element_type=jnp.float32)
        columns = pl.ds(pl.multiple_of(b * width, width), width)
        product[b] = localized * ens_ref[:, columns].astype(jnp.float32)
        return carry

    lax.fori_loop(0, blocks, spread, 0, unroll=min(blocks, 8))
    product[blocks] = jnp.zeros((rows, width), jnp.float32)
    lane = lax.broadcasted_iota(jnp.int32, (rows, width), 1)

    def place(owner, block, shift, size):
        both = jnp.where(lane >= shift, product[block], product[block + 1])
        turned = pltpu.roll(both, (width - shift) % width, 1)
        kept = jnp.where(lane < size, turned, 0.0)
        out_ref[owner % inner, owner // inner] = kept.astype(jnp.bfloat16)

    region_loop(sizes_ref, owner_ref, width, place)


def scale_kernel(
    inner, sizes_ref, owner_ref, cot_ref, ens_ref, out_ref, columns_of
):
    width = cot_ref.shape[3]
    rows = ens_ref.shape[0]
    blocks = ens_ref.shape[1] // width
    lane = lax.broadcasted_iota(jnp.int32, (rows, width), 1)
    columns_of[0] = jnp.zeros((rows, width), jnp.float32)

    def place(owner, block, shift, size):
        region = cot_ref[owner % inner, owner // inner].astype(jnp.float32)
        turned = pltpu.roll(region, shift, 1)
        columns_of[block] = jnp.where(lane >= shift, turned, columns_of[block])
        columns_of[block + 1] = turned

    region_loop(sizes_ref, owner_ref, width, place)
    for b in range(blocks):
        part = slice(b * width, (b + 1) * width)
        out_ref[:, part] = (ens_ref[:, part].astype(jnp.float32) * columns_of[b]).astype(
            jnp.bfloat16
        )


def backward_kernel(
    pattern_ref, scaled_ref, halo_ref, up_ref, htile_ref, out_ref, mixed, total
):
    blocks, slots = pattern_ref.shape
    rows = scaled_ref.shape[0]
    width = htile_ref.shape[1]
    extended = jnp.concatenate([scaled_ref[...], halo_ref[...]], axis=0)
    dims = (((0,), (0,)), ((), ()))
    summed = lax.dot_general(up_ref[0], extended, dims, preferred_element_type=jnp.float32)
    summed = summed + lax.dot_general(
        up_ref[1], extended, dims, preferred_element_type=jnp.float32
    )
    for b in range(blocks):
        mixed[b] = summed[:, b * width : (b + 1) * width].astype(jnp.bfloat16)
        total[b] = jnp.zeros((rows, width), jnp.float32)

    def gather(b, carry):
        spread = lax.dot_general(
            mixed[b], htile_ref[...], (((1,), (1,)), ((), ())), preferred_element_type=jnp.float32
        )
        for k in range(slots):
            target = pattern_ref[b, k]
            total[target] = total[target] + spread[:, k * width : (k + 1) * width]
        return carry

    lax.fori_loop(0, blocks, gather, 0, unroll=min(blocks, 8))
    for b in range(blocks):
        out_ref[:, b * width : (b + 1) * width] = total[b].astype(jnp.bfloat16)


def sum_kernel(scale, parts_ref, out_ref):
    total = parts_ref[0].astype(jnp.float32)
    for i in range(1, parts_ref.shape[0]):
        total = total + parts_ref[i].astype(jnp.float32)
    out_ref[...] = (total * scale).astype(jnp.bfloat16)


def body(alpha, ens, htile, vloc, pattern, region_sizes, owner, cotangent):
    reach = VREACH
    members, fields, levels, columns = alpha.shape
    assert members == 1
    slots, width, _ = htile.shape
    blocks = columns // width
    region_max = cotangent.shape[2]
    assert region_max == width
    wide = lax.axis_size("wide")
    slabs = lax.axis_size("lev")
    inner = next(i for i in range(math.isqrt(wide), wide + 1) if wide % i == 0)
    outer = wide // inner
    lines = [[o * inner + i for o in range(outer)] for i in range(inner)]
    planes = [[o * inner + i for i in range(inner)] for o in range(outer)]
    rows = fields * levels
    halo = fields * reach
    member_scale = 1.0 / math.sqrt(members * wide)

    cot_rows = cotangent.reshape(1, rows, region_max)
    cot_line = lax.all_to_all(
        jnp.broadcast_to(cot_rows, (outer, rows, region_max)),
        "wide", 0, 0, axis_index_groups=lines, tiled=True,
    )

    def halo_of(block):
        below, above = halo_swap(
            block[:, levels - reach :, :].reshape(halo, columns),
            block[:, :reach, :].reshape(halo, columns),
            "lev",
        )
        return jnp.concatenate([below, above], axis=0)

    alpha_rows = alpha.reshape(rows, columns)
    ens_rows = ens.reshape(rows, columns)
    stacked = htile.reshape(slots * width, width)
    span = rows + 2 * halo
    down, up = pl.pallas_call(
        functools.partial(weight_kernel, fields, slabs),
        out_shape=(
            jax.ShapeDtypeStruct((2, rows, span), jnp.bfloat16),
            jax.ShapeDtypeStruct((2, span, rows), jnp.bfloat16),
        ),
        in_specs=[VMEM],
        out_specs=(VMEM, VMEM),
        scratch_shapes=[pltpu.VMEM((vloc.shape[0] + 2 * SUB, vloc.shape[1]), jnp.float32)],
        name="weights",
    )(vloc)

    products = pl.pallas_call(
        functools.partial(forward_kernel, inner),
        out_shape=jax.ShapeDtypeStruct((inner, outer, rows, width), jnp.bfloat16),
        in_specs=[SMEM] * 3 + [VMEM] * 5,
        out_specs=VMEM,
        scratch_shapes=[
            pltpu.VMEM((blocks, rows, width), jnp.bfloat16),
            pltpu.VMEM((blocks + 1, rows, width), jnp.float32),
        ],
        cost_estimate=pl.CostEstimate(flops=10**9, bytes_accessed=2 << 20, transcendentals=0),
        name="forward",
    )(pattern, region_sizes, owner, alpha_rows, halo_of(alpha[0]), down, ens_rows, stacked)

    merged = jnp.concatenate(
        [products, jnp.broadcast_to(cot_line[None], (inner,) + cot_line.shape)], axis=1
    )
    arrived = lax.all_to_all(merged, "wide", 0, 0, axis_index_groups=planes, tiled=True)
    partial = pl.pallas_call(
        functools.partial(sum_kernel, 1.0),
        grid=(1,),
        out_shape=jax.ShapeDtypeStruct((outer, rows, width), jnp.bfloat16),
        in_specs=[pl.BlockSpec((inner, outer, rows, width), lambda i: (0, 0, 0, 0))],
        out_specs=pl.BlockSpec((outer, rows, width), lambda i: (0, 0, 0)),
        name="partial",
    )(arrived)
    terms = lax.all_to_all(partial, "wide", 0, 0, axis_index_groups=lines, tiled=True)

    scaled = pl.pallas_call(
        functools.partial(scale_kernel, inner),
        grid=(1,),
        out_shape=jax.ShapeDtypeStruct((rows, columns), jnp.bfloat16),
        in_specs=[
            SMEM,
            SMEM,
            pl.BlockSpec((inner, outer, rows, width), lambda i: (0, 1, 0, 0)),
            pl.BlockSpec((rows, columns), lambda i: (0, 0)),
        ],
        out_specs=pl.BlockSpec((rows, columns), lambda i: (0, 0)),
        scratch_shapes=[pltpu.VMEM((blocks + 1, rows, width), jnp.float32)],
        cost_estimate=pl.CostEstimate(flops=10**7, bytes_accessed=1 << 20, transcendentals=0),
        name="scale",
    )(region_sizes, owner, arrived, ens_rows)
    gradient = pl.pallas_call(
        backward_kernel,
        out_shape=jax.ShapeDtypeStruct((rows, columns), jnp.bfloat16),
        in_specs=[SMEM] + [VMEM] * 4,
        out_specs=VMEM,
        scratch_shapes=[
            pltpu.VMEM((blocks, rows, width), jnp.bfloat16),
            pltpu.VMEM((blocks, rows, width), jnp.float32),
        ],
        cost_estimate=pl.CostEstimate(flops=10**9, bytes_accessed=1 << 20, transcendentals=0),
        name="backward",
    )(pattern, scaled, halo_of(scaled.reshape(fields, levels, columns)), up, stacked)

    increment = pl.pallas_call(
        functools.partial(sum_kernel, member_scale),
        out_shape=jax.ShapeDtypeStruct((rows, width), jnp.bfloat16),
        in_specs=[VMEM],
        out_specs=VMEM,
        name="total",
    )(terms)
    return (
        increment.reshape(fields, levels, width),
        gradient.reshape(members, fields, levels, columns),
    )


def solution(mesh):
    placed = (
        P("wide", None, "lev", None),
        P("wide", None, "lev", None),
        P(),
        P(),
        P(),
        P(),
        P(),
        P(None, "lev", "wide"),
    )
    return jax.shard_map(
        body,
        mesh=mesh,
        in_specs=placed,
        out_specs=(P(None, "lev", "wide"), P("wide", None, "lev", None)),
        check_vma=False,
    )
```

time: 149 us -> 54 us (0.36)
  local copies, waits for them, and re-layouts: 54.2 us -> 5.11 us
  waiting for transfers between devices: 33.7 us -> 2.9 us
  other arithmetic: 27.8 us -> 1.36 us
  blocking collectives: 0 us -> 17.5 us
  Pallas kernels: 0 us -> 13.7 us
  starting transfers between devices: 25.2 us -> 11.9 us
  matrix products: 5.5 us -> 0 us
    all_to_all x3 -> x2, waiting for transfers between devices: 33.5 us -> 2.89 us  [the longest x1 2.89 us: body(): lax.all_to_all(partial, 'wide', 0, 0, axis_index_groups=lines, tiled=True)]
    gather x10 -> x0, local copies, waits for them, and re-layouts: 25.2 us -> none  [the longest x2 10.3 us: body(): ens_slots = jnp.take(ens, source, axis=3) * keep_mask]
    all_to_all x0 -> x1, blocking collectives: none -> 17.5 us  [body(): lax.all_to_all(merged, 'wide', 0, 0, axis_index_groups=planes, tiled=True)]
    pallas_call x0 -> x6, Pallas kernels: none -> 13.7 us  [the longest x1 3.4 us: body(): pl.pallas_call(functools.partial(forward_kernel, inner), out_shape=jax.Sh...]
    unnamed x73 -> x9, local copies, waits for them, and re-layouts: 16 us -> 2.47 us
    and x2 -> x0, other arithmetic: 11.9 us -> none  [the longest x1 11.8 us: body(): scaled = jnp.take(returned, slot_of, axis=3)]
    gather x5 -> x0, other arithmetic: 9.11 us -> none  [the longest x2 4.53 us: slot_tables(): owner[region_of] * region_max + column_ids - region_starts[region_of]]
    ppermute x4 -> x2, starting transfers between devices: 8.64 us -> 0.63 us  [halo_swap(): lax.ppermute(jnp.stack([rows_top, rows_bottom]), axis, [(0, 1), (1, 0)])]
  transfers between devices with their start and end apart: 7 -> 4, of which waited for: 4 -> 1; matrix products, arithmetic and copies ran while one was open for 33% -> 5% of each run, Pallas kernels for 0% -> 18%
where the time goes in v1:
time: 54 us; the launch traced here: 53.2 us
  blocking collectives  17.5 us (32%)
  Pallas kernels  13.7 us (25%)
  starting transfers between devices  11.9 us (22%)
  local copies, waits for them, and re-layouts  5.11 us (9%)
  waiting for transfers between devices  2.9 us (5%)
  other arithmetic  1.36 us (3%)
  between operations  0.72 us (1%)
    all_to_all x1, blocking collectives, body(): lax.all_to_all(merged, 'wide', 0, 0, axis_index_groups=planes, tiled=True)  17.5 us
    all_to_all x1, starting transfers between devices, body(): lax.all_to_all(jnp.broadcast_to(cot_rows, (outer, rows, region_max)), 'wi...  6.48 us
    all_to_all x1, starting transfers between devices, body(): lax.all_to_all(partial, 'wide', 0, 0, axis_index_groups=lines, tiled=True)  4.81 us
    pallas_call x1, Pallas kernels, body(): pl.pallas_call(functools.partial(forward_kernel, inner), out_shape=jax.Sh...  3.4 us
    pallas_call x1, Pallas kernels, body(): pl.pallas_call(backward_kernel, out_shape=jax.ShapeDtypeStruct((rows, col...  2.9 us
    all_to_all x1, waiting for transfers between devices, body(): lax.all_to_all(partial, 'wide', 0, 0, axis_index_groups=lines, tiled=True)  2.89 us
    unnamed x9, local copies, waits for them, and re-layouts  2.47 us
    pallas_call x1, Pallas kernels, body(): pl.pallas_call(functools.partial(scale_kernel, inner), grid=(1,), out_sha...  2.41 us
  transfers between devices with their start and end apart: 4, of which 1 were waited for; matrix products, arithmetic and copies ran while one was open for 5% of the time, Pallas kernels for 18%

profile of v1, /device:TPU:0, one launch (start us, length us, event | category | flops | bytes accessed | tf_op | source)
XLA Modules:
  0.0 53.2 jit_solution(13112650467093148048)
XLA Ops:
  0.6 0.9 %fusion.1 = (bf16[4,4,1024]{2,1,0:T(4,128)(2,1)S(1)}, bf16[4,4,1024]{2,1,0:T(4,128)(2,1)S(1)}) fusion(bf16[4,32,1024]{2,1,0:T(8,128)(2,1)} %bitcast.21), kind=kLoop, calls=%fused_computation.10 | loop fusion | bytes 131072 | tf_op jit(solution)/shard_map/slice | solution.py:220
  1.6 0.0 copy-start.2
  1.6 0.6 %collective-permute-start = (bf16[2,16,1024]{2,1,0:T(8,128)(2,1)S(1)}, bf16[2,16,1024]{2,1,0:T(8,128)(2,1)S(1)}, u32[]{:S(2)}, u32[]{:S(2)}) collective-permute-start(bf16[2,16,1024]{2,1,0:T(8,128)(2,1)S(1)} %pad_maximum_fusion.1), channel_id=1, source_target_pairs={{0,1},{1,0},{2,3},{3,2},{4,5},{5,4},{6,7},{7,6},{8,9},{9,8},{10,11... | collective-permute-start | bytes 196616 | tf_op jit(solution)/shard_map/ppermute | solution.py:20
  2.2 0.2 copy-done.2
  2.3 0.7 %broadcast_in_dim.14 = bf16[4,128,128]{2,1,0:T(8,128)(2,1)} broadcast(bf16[128,128]{1,0:T(8,128)(2,1)S(1)} %bitcast.19), dimensions={1,2} | broadcast | bytes 163840 | tf_op jit(solution)/shard_map/broadcast_in_dim | solution.py:214
  3.0 0.0 copy-start.3
  3.0 6.5 %all-to-all-start = ((bf16[4,128,128]{2,1,0:T(8,128)(2,1)}), bf16[4,128,128]{2,1,0:T(8,128)(2,1)S(1)}, u32[]{:S(2)}, u32[]{:S(2)}) async-start(bf16[4,128,128]{2,1,0:T(8,128)(2,1)} %broadcast_in_dim.14), calls=%async_computation | async-start | bytes 262144 | tf_op jit(solution)/shard_map/all_to_all | solution.py:213
  9.5 0.0 copy-done.3
  9.5 0.7 %copy.10.vloc_ref = f32[64,9]{1,0:T(8,128)} copy(f32[64,9]{0,1:T(8,128)S(1)} %copy-done.3) | data formatting | bytes 4608 | tf_op args[3]
  10.2 1.7 %weights.1 = (bf16[2,128,160]{2,1,0:T(8,128)(2,1)}, bf16[2,160,128]{2,1,0:T(8,128)(2,1)}) custom-call(f32[64,9]{1,0:T(8,128)} %copy.10.vloc_ref), custom_call_target="tpu_custom_call" | custom-call | tf_op jit(solution)/shard_map/weights/pallas_call | solution.py:230
  11.9 0.0 collective-permute-done
  11.9 0.6 %pad_maximum_fusion.2.halo_ref = bf16[32,1024]{1,0:T(8,128)(2,1)} fusion(bf16[16,1024]{1,0:T(8,128)(2,1)S(1)} %get-tuple-element.13, bf16[16,1024]{1,0:T(8,128)(2,1)S(1)} %get-tuple-element.12), kind=kLoop, calls=%fused_computation.2 | loop fusion | flops 131072 | bytes 131072 | tf_op jit(solution)/shard_map/concatenate | solution.py:224
  12.6 3.4 %forward.1 = bf16[4,4,128,128]{3,2,1,0:T(8,128)(2,1)} custom-call(s32[8,8]{1,0:T(8,128)} %pattern_ref.3, s32[16]{0:T(128)} %sizes_ref.3, s32[16]{0:T(128)} %owner_ref.3, bf16[128,1024]{1,0:T(8,128)(2,1)} %bitcast.22, bf16[32,1024]{1,0:T(8,128)(2,1)} %pad_maximum_fusion.2.halo_ref, bf16[2,128,160]{2,1,0:T(8,128)(2,1)} %get-tuple-element.4.down_ref, ...), custom_call_target="tpu_custom_call" | custom-call | flops 1000000000 | bytes 2097152 | tf_op jit(solution)/shard_map/forward/pallas_call | solution.py:242
  16.0 0.0 copy-start.1
  16.0 0.0 all-to-all-done
  16.0 0.1 broadcast_in_dim.15
  16.1 0.9 %copy-done.1 = bf16[4,4,128,128]{3,2,1,0:T(8,128)(2,1)S(1)} copy-done((bf16[4,4,128,128]{3,2,1,0:T(8,128)(2,1)S(1)}, bf16[4,4,128,128]{3,2,1,0:T(8,128)(2,1)}, u32[]{:S(2)}) %copy-start.1) | copy-done | bytes 524312
  17.0 0.1 pad_maximum_fusion
  17.1 17.5 %all_to_all.15.parts_ref.cot_ref = bf16[4,8,128,128]{3,2,1,0:T(8,128)(2,1)} all-to-all(bf16[4,8,128,128]{3,2,1,0:T(8,128)(2,1)S(1)} %pad_maximum_fusion), channel_id=1, replica_groups={{0,2,4,6},{8,10,12,14},{16,18,20,22},{24,26,28,30},{1,3,5,7},{9,11,13,1..., dimensions={0} | all-to-all | bytes 2097152 | tf_op jit(solution)/shard_map/all_to_all | solution.py:258
  34.6 2.4 %scale.1.scaled_ref = bf16[128,1024]{1,0:T(8,128)(2,1)} custom-call(s32[16]{0:T(128)} %sizes_ref.3, s32[16]{0:T(128)} %owner_ref.3, bf16[4,8,128,128]{3,2,1,0:T(8,128)(2,1)} %all_to_all.15.parts_ref.cot_ref, bf16[128,1024]{1,0:T(8,128)(2,1)} %bitcast.18), custom_call_target="tpu_custom_call" | custom-call | flops 10000000 | bytes 1048576 | tf_op jit(solution)/shard_map/scale/pallas_call | solution.py:269
  37.0 0.9 %fusion = (bf16[4,4,1024]{2,1,0:T(4,128)(2,1)S(1)}, bf16[4,4,1024]{2,1,0:T(4,128)(2,1)S(1)}) fusion(bf16[4,32,1024]{2,1,0:T(8,128)(2,1)} %bitcast.16), kind=kLoop, calls=%fused_computation.9 | loop fusion | bytes 131072 | tf_op jit(solution)/shard_map/slice | solution.py:220
  38.0 0.1 collective-permute-start.1
  38.0 1.8 %partial.1 = bf16[4,128,128]{2,1,0:T(8,128)(2,1)} custom-call(bf16[4,8,128,128]{3,2,1,0:T(8,128)(2,1)} %all_to_all.15.parts_ref.cot_ref), custom_call_target="tpu_custom_call" | custom-call | tf_op jit(solution)/shard_map/partial/pallas_call | solution.py:259
  39.8 4.8 %all-to-all-start.2 = ((bf16[4,128,128]{2,1,0:T(8,128)(2,1)}), bf16[4,128,128]{2,1,0:T(8,128)(2,1)S(1)}, u32[]{:S(2)}, u32[]{:S(2)}) async-start(bf16[4,128,128]{2,1,0:T(8,128)(2,1)} %partial.1), calls=%async_computation.2 | async-start | bytes 262144 | tf_op jit(solution)/shard_map/all_to_all | solution.py:267
  44.6 0.0 collective-permute-done.1
  44.6 0.6 %pad_maximum_fusion.4.halo_ref = bf16[32,1024]{1,0:T(8,128)(2,1)} fusion(bf16[16,1024]{1,0:T(8,128)(2,1)S(1)} %get-tuple-element.11, bf16[16,1024]{1,0:T(8,128)(2,1)S(1)} %get-tuple-element.10), kind=kLoop, calls=%fused_computation.4 | loop fusion | flops 131072 | bytes 131072 | tf_op jit(solution)/shard_map/concatenate | solution.py:224
  45.2 2.9 %backward.1 = bf16[128,1024]{1,0:T(8,128)(2,1)} custom-call(s32[8,8]{1,0:T(8,128)} %pattern_ref.3, bf16[128,1024]{1,0:T(8,128)(2,1)} %scale.1.scaled_ref, bf16[32,1024]{1,0:T(8,128)(2,1)} %pad_maximum_fusion.4.halo_ref, bf16[2,160,128]{2,1,0:T(8,128)(2,1)} %get-tuple-element.5.up_ref, bf16[1024,128]{1,0:T(8,128)(2,1)} %bitcast.24), custom_call_target="tpu_custom_call" | custom-call | flops 1000000000 | bytes 1048576 | tf_op jit(solution)/shard_map/backward/pallas_call | solution.py:284
  48.1 2.9 %all-to-all-done.2.parts_ref = bf16[4,128,128]{2,1,0:T(8,128)(2,1)S(1)} async-done(((bf16[4,128,128]{2,1,0:T(8,128)(2,1)}), bf16[4,128,128]{2,1,0:T(8,128)(2,1)S(1)}, u32[]{:S(2)}, u32[]{:S(2)}) %all-to-all-start.2) | async-done | bytes 131104 | tf_op jit(solution)/shard_map/all_to_all | solution.py:267
  51.0 0.0 copy-start
  51.0 0.6 %copy-done = bf16[4,128,128]{2,1,0:T(8,128)(2,1)} copy-done((bf16[4,128,128]{2,1,0:T(8,128)(2,1)}, bf16[4,128,128]{2,1,0:T(8,128)(2,1)S(1)}, u32[]{:S(2)}) %copy-start) | copy-done | bytes 131096
  51.7 1.5 %total.1 = bf16[128,128]{1,0:T(8,128)(2,1)} custom-call(bf16[4,128,128]{2,1,0:T(8,128)(2,1)} %copy-done), custom_call_target="tpu_custom_call" | custom-call | tf_op jit(solution)/shard_map/total/pallas_call | solution.py:297
  (8 shorter events, 0.1 us)
Async XLA Ops:
  1.6 0.8 %copy-start.2 = (bf16[4,32,128]{2,1,0:T(8,128)(2,1)S(1)}, bf16[4,32,128]{2,1,0:T(8,128)(2,1)}, u32[]{:S(2)}) copy-start(bf16[4,32,128]{2,1,0:T(8,128)(2,1)} %param.15) | copy-start | bytes 98308
  1.6 10.3 %collective-permute-start = (bf16[2,16,1024]{2,1,0:T(8,128)(2,1)S(1)}, bf16[2,16,1024]{2,1,0:T(8,128)(2,1)S(1)}, u32[]{:S(2)}, u32[]{:S(2)}) collective-permute-start(bf16[2,16,1024]{2,1,0:T(8,128)(2,1)S(1)} %pad_maximum_fusion.1), channel_id=1, source_target_pairs={{0,1},{1,0},{2,3},{3,2},{4,5},{5,4},{6,7},{7,6},{8,9},{9,8},{10,11... | collective-permute-start | bytes 196616 | tf_op jit(solution)/shard_map/ppermute | solution.py:20
  3.0 6.5 %copy-start.3 = (f32[64,9]{0,1:T(8,128)S(1)}, f32[64,9]{0,1:T(8,128)}, u32[]{:S(2)}) copy-start(f32[64,9]{0,1:T(8,128)} %param.11) | copy-start | bytes 6916
  3.0 12.9 %all-to-all-start = ((bf16[4,128,128]{2,1,0:T(8,128)(2,1)}), bf16[4,128,128]{2,1,0:T(8,128)(2,1)S(1)}, u32[]{:S(2)}, u32[]{:S(2)}) async-start(bf16[4,128,128]{2,1,0:T(8,128)(2,1)} %broadcast_in_dim.14), calls=%async_computation | async-start | bytes 262144 | tf_op jit(solution)/shard_map/all_to_all | solution.py:213
  16.0 1.0 %copy-start.1 = (bf16[4,4,128,128]{3,2,1,0:T(8,128)(2,1)S(1)}, bf16[4,4,128,128]{3,2,1,0:T(8,128)(2,1)}, u32[]{:S(2)}) copy-start(bf16[4,4,128,128]{3,2,1,0:T(8,128)(2,1)} %forward.1) | copy-start | bytes 1572868
  38.0 6.7 %collective-permute-start.1 = (bf16[2,16,1024]{2,1,0:T(8,128)(2,1)S(1)}, bf16[2,16,1024]{2,1,0:T(8,128)(2,1)S(1)}, u32[]{:S(2)}, u32[]{:S(2)}) collective-permute-start(bf16[2,16,1024]{2,1,0:T(8,128)(2,1)S(1)} %pad_maximum_fusion.3), channel_id=1, source_target_pairs={{0,1},{1,0},{2,3},{3,2},{4,5},{5,4},{6,7},{7,6},{8,9},{9,8},{10,11... | collective-permute-start | bytes 196616 | tf_op jit(solution)/shard_map/ppermute | solution.py:20
  39.8 11.2 %all-to-all-start.2 = ((bf16[4,128,128]{2,1,0:T(8,128)(2,1)}), bf16[4,128,128]{2,1,0:T(8,128)(2,1)S(1)}, u32[]{:S(2)}, u32[]{:S(2)}) async-start(bf16[4,128,128]{2,1,0:T(8,128)(2,1)} %partial.1), calls=%async_computation.2 | async-start | bytes 262144 | tf_op jit(solution)/shard_map/all_to_all | solution.py:267
  51.0 0.7 %copy-start = (bf16[4,128,128]{2,1,0:T(8,128)(2,1)}, bf16[4,128,128]{2,1,0:T(8,128)(2,1)S(1)}, u32[]{:S(2)}) copy-start(bf16[4,128,128]{2,1,0:T(8,128)(2,1)S(1)} %all-to-all-done.2.parts_ref) | copy-start | bytes 393220

commit v2 on v1

v2 whole, which is shorter than its diff:
```python
import functools
import math

import jax
import jax.numpy as jnp
from jax import lax
from jax.experimental import pallas as pl
from jax.experimental.pallas import tpu as pltpu
from jax.sharding import PartitionSpec as P


VREACH = 4
LANES = 128
VMEM = pl.BlockSpec(memory_space=pltpu.VMEM)
SMEM = pl.BlockSpec(memory_space=pltpu.SMEM)


def neighbour_slabs(block):
    count = lax.axis_size("lev")
    if count == 2:
        return [lax.ppermute(block, "lev", [(0, 1), (1, 0)])]
    return [
        lax.ppermute(block, "lev", [(i, i + 1) for i in range(count - 1)]),
        lax.ppermute(block, "lev", [(i + 1, i) for i in range(count - 1)]),
    ]


def slab_steps(slabs):
    if slabs == 2:
        return [0, 1 - 2 * lax.axis_index("lev")]
    return [0, -1, 1]


def split_bf16(value):
    high = value.astype(jnp.bfloat16)
    return high, (value - high.astype(jnp.float32)).astype(jnp.bfloat16)


def weight_kernel(fields, slabs, vloc_ref, down_ref, up_ref, taps):
    slab = lax.axis_index("lev")
    reach = VREACH
    levels = vloc_ref.shape[1] // slabs
    rows = fields * levels
    taps[...] = jnp.zeros_like(taps)
    taps[: vloc_ref.shape[0], : vloc_ref.shape[1]] = vloc_ref[...]
    lane = lax.broadcasted_iota(jnp.int32, taps.shape, 1)

    def slab_weights(step):
        first = (slab + step) * levels
        turned = pltpu.roll(taps[...], lax.rem(2 * LANES - first, LANES), 1)
        once = jnp.where(lane < levels, turned, 0.0)
        total = once
        for field in range(1, fields):
            total = total + pltpu.roll(once, field * levels, 1)
        return total

    row = lax.broadcasted_iota(jnp.int32, (rows, rows), 0)
    col = lax.broadcasted_iota(jnp.int32, (rows, rows), 1)
    same = (row // levels) == (col // levels)
    own = slab_weights(0)

    def band(weights, shift, valid):
        total = jnp.zeros((rows, rows), jnp.float32)
        for tap in range(2 * reach + 1):
            line = jnp.broadcast_to(weights[tap : tap + 1, :rows], (rows, rows))
            total = jnp.where(shift == tap - reach, line, total)
        return split_bf16(jnp.where(same & valid, total, 0.0))

    for i, step in enumerate(slab_steps(slabs)):
        valid = (slab + step >= 0) & (slab + step < slabs)
        part = slice(i * rows, (i + 1) * rows)
        offset = step * levels
        down_ref[0, part, :], down_ref[1, part, :] = band(own, row + offset - col, valid)
        up_ref[0, :, part], up_ref[1, :, part] = band(
            own if i == 0 else slab_weights(step), row - col - offset, valid
        )


def region_loop(sizes_ref, owner_ref, width, body):
    def step(region, start):
        size = sizes_ref[region]
        body(owner_ref[region], start // width, start % width, size)
        return start + size

    lax.fori_loop(0, sizes_ref.shape[0], step, jnp.int32(0), unroll=4)


def forward_kernel(grid, pattern_ref, sizes_ref, owner_ref, down_ref, ens_ref, htile_ref, *refs):
    outer, inner = grid
    out_refs = refs[-inner - 3 : -3]
    slab_refs = refs[: -inner - 3]
    mixed, product, placed = refs[-3:]
    blocks, slots = pattern_ref.shape
    rows = ens_ref.shape[0]
    width = htile_ref.shape[1]
    extended = jnp.concatenate([ref[...] for ref in slab_refs], axis=0)
    dims = (((0,), (0,)), ((), ()))
    summed = lax.dot_general(down_ref[0], extended, dims, preferred_element_type=jnp.float32)
    summed = summed + lax.dot_general(
        down_ref[1], extended, dims, preferred_element_type=jnp.float32
    )
    for b in range(blocks):
        mixed[b] = summed[:, b * width : (b + 1) * width].astype(jnp.bfloat16)

    def spread(b, carry):
        picked = jnp.concatenate([mixed[pattern_ref[b, k]] for k in range(slots)], axis=1)
        localized = jnp.dot(picked, htile_ref[...], preferred_element_type=jnp.float32)
        columns = pl.ds(pl.multiple_of(b * width, width), width)
        product[b] = localized * ens_ref[:, columns].astype(jnp.float32)
        return carry

    lax.fori_loop(0, blocks, spread, 0, unroll=min(blocks, 8))
    product[blocks] = jnp.zeros((rows, width), jnp.float32)
    lane = lax.broadcasted_iota(jnp.int32, (rows, width), 1)
    me = lax.axis_index("wide")
    here, line = me % inner, me // inner

    def place(owner, block, shift, size):
        both = jnp.where(lane >= shift, product[block], product[block + 1])
        turned = pltpu.roll(both, (width - shift) % width, 1)
        kept = jnp.where(lane < size, turned, 0.0).astype(jnp.bfloat16)
        placed[(owner % inner - here + inner) % inner, (owner // inner - line + outer) % outer] = kept

    region_loop(sizes_ref, owner_ref, width, place)
    for i in range(inner):
        out_refs[i][...] = placed[i]


def scale_kernel(grid, sizes_ref, owner_ref, ens_ref, *refs):
    outer, inner = grid
    cot_refs = refs[:inner]
    out_ref, gathered, columns_of = refs[inner:]
    rows, width = cot_refs[0].shape[1:]
    blocks = ens_ref.shape[1] // width
    lane = lax.broadcasted_iota(jnp.int32, (rows, width), 1)
    me = lax.axis_index("wide")
    here, line = me % inner, me // inner
    for i in range(inner):
        gathered[i] = cot_refs[i][...]
    columns_of[0] = jnp.zeros((rows, width), jnp.float32)

    def place(owner, block, shift, size):
        region = gathered[(here - owner % inner + inner) % inner, (line - owner // inner + outer) % outer]
        turned = pltpu.roll(region.astype(jnp.float32), shift, 1)
        columns_of[block] = jnp.where(lane >= shift, turned, columns_of[block])
        columns_of[block + 1] = turned

    region_loop(sizes_ref, owner_ref, width, place)
    for b in range(blocks):
        part = slice(b * width, (b + 1) * width)
        out_ref[:, part] = (ens_ref[:, part].astype(jnp.float32) * columns_of[b]).astype(
            jnp.bfloat16
        )


def backward_kernel(pattern_ref, up_ref, htile_ref, *refs):
    slab_refs = refs[:-3]
    out_ref, mixed, total = refs[-3:]
    blocks, slots = pattern_ref.shape
    rows = out_ref.shape[0]
    width = htile_ref.shape[1]
    extended = jnp.concatenate([ref[...] for ref in slab_refs], axis=0)
    summed = jnp.dot(up_ref[0], extended, preferred_element_type=jnp.float32)
    summed = summed + jnp.dot(up_ref[1], extended, preferred_element_type=jnp.float32)
    for b in range(blocks):
        mixed[b] = summed[:, b * width : (b + 1) * width].astype(jnp.bfloat16)
        total[b] = jnp.zeros((rows, width), jnp.float32)

    def gather(b, carry):
        spread = lax.dot_general(
            mixed[b], htile_ref[...], (((1,), (1,)), ((), ())), preferred_element_type=jnp.float32
        )
        for k in range(slots):
            target = pattern_ref[b, k]
            total[target] = total[target] + spread[:, k * width : (k + 1) * width]
        return carry

    lax.fori_loop(0, blocks, gather, 0, unroll=min(blocks, 8))
    for b in range(blocks):
        out_ref[:, b * width : (b + 1) * width] = total[b].astype(jnp.bfloat16)


def partial_kernel(*refs):
    count = refs[0].shape[0]
    parts, outs = refs[:-count], refs[-count:]
    for i in range(count):
        total = parts[0][i].astype(jnp.float32)
        for part in parts[1:]:
            total = total + part[i].astype(jnp.float32)
        outs[i][...] = total.astype(outs[i].dtype)


def total_kernel(scale, *refs):
    total = refs[0][...].astype(jnp.float32)
    for part in refs[1:-1]:
        total = total + part[...].astype(jnp.float32)
    refs[-1][...] = (total * scale).astype(jnp.bfloat16)


def cost(flops, moved):
    return pl.CostEstimate(flops=flops, bytes_accessed=moved, transcendentals=0)


def body(alpha, ens, htile, vloc, pattern, region_sizes, owner, cotangent):
    members, fields, levels, columns = alpha.shape
    assert members == 1
    slots, width, _ = htile.shape
    blocks = columns // width
    assert cotangent.shape[2] == width == LANES
    wide = lax.axis_size("wide")
    slabs = lax.axis_size("lev")
    inner = next(i for i in range(math.isqrt(wide), wide + 1) if wide % i == 0)
    outer = wide // inner
    grid = (outer, inner)
    rows = fields * levels
    span = rows * len(slab_steps(slabs))
    member_scale = 1.0 / math.sqrt(members * wide)
    bf16 = functools.partial(jax.ShapeDtypeStruct, dtype=jnp.bfloat16)

    def along_line(value, step):
        pairs = [
            (o * inner + i, (o + step) % outer * inner + i)
            for o in range(outer)
            for i in range(inner)
        ]
        return lax.ppermute(value, "wide", pairs)

    def in_plane(value, step):
        pairs = [
            (o * inner + i, o * inner + (i + step) % inner)
            for o in range(outer)
            for i in range(inner)
        ]
        return lax.ppermute(value, "wide", pairs)

    alpha_rows = alpha.reshape(rows, columns)
    ens_rows = ens.reshape(rows, columns)
    stacked = htile.reshape(slots * width, width)
    alpha_slabs = [alpha_rows] + neighbour_slabs(alpha_rows)

    cot_rows = cotangent.reshape(rows, width)
    cot_line = jnp.stack([cot_rows] + [along_line(cot_rows, i) for i in range(1, outer)])
    cot_parts = [cot_line] + [in_plane(cot_line, i) for i in range(1, inner)]

    down, up = pl.pallas_call(
        functools.partial(weight_kernel, fields, slabs),
        out_shape=(bf16((2, span, rows)), bf16((2, rows, span))),
        in_specs=[VMEM],
        out_specs=(VMEM, VMEM),
        scratch_shapes=[pltpu.VMEM((2 * 8, LANES), jnp.float32)],
        cost_estimate=cost(10**6, 10**5),
        name="weights",
    )(vloc.T)

    sent = pl.pallas_call(
        functools.partial(forward_kernel, grid),
        out_shape=[bf16((outer, rows, width))] * inner,
        in_specs=[SMEM] * 3 + [VMEM] * (3 + len(alpha_slabs)),
        out_specs=[VMEM] * inner,
        scratch_shapes=[
            pltpu.VMEM((blocks, rows, width), jnp.bfloat16),
            pltpu.VMEM((blocks + 1, rows, width), jnp.float32),
            pltpu.VMEM((inner, outer, rows, width), jnp.bfloat16),
        ],
        cost_estimate=cost(10**9, 2 << 20),
        name="forward",
    )(pattern, region_sizes, owner, down, ens_rows, stacked, *alpha_slabs)

    arrived = [sent[0]] + [in_plane(sent[i], i) for i in range(1, inner)]
    partial = pl.pallas_call(
        partial_kernel,
        out_shape=[bf16((rows, width))] * outer,
        in_specs=[VMEM] * inner,
        out_specs=[VMEM] * outer,
        cost_estimate=cost(10**6, 1 << 20),
        name="partial",
    )(*arrived)
    terms = [partial[0]] + [along_line(partial[i], i) for i in range(1, outer)]

    scaled = pl.pallas_call(
        functools.partial(scale_kernel, grid),
        out_shape=bf16((rows, columns)),
        in_specs=[SMEM] * 2 + [VMEM] * (1 + inner),
        out_specs=VMEM,
        scratch_shapes=[
            pltpu.VMEM((inner, outer, rows, width), jnp.bfloat16),
            pltpu.VMEM((blocks + 1, rows, width), jnp.float32),
        ],
        cost_estimate=cost(10**7, 1 << 20),
        name="scale",
    )(region_sizes, owner, ens_rows, *cot_parts)
    scaled_slabs = [scaled] + neighbour_slabs(scaled)
    gradient = pl.pallas_call(
        backward_kernel,
        out_shape=bf16((rows, columns)),
        in_specs=[SMEM] + [VMEM] * (2 + len(scaled_slabs)),
        out_specs=VMEM,
        scratch_shapes=[
            pltpu.VMEM((blocks, rows, width), jnp.bfloat16),
            pltpu.VMEM((blocks, rows, width), jnp.float32),
        ],
        cost_estimate=cost(10**9, 1 << 20),
        name="backward",
    )(pattern, up, stacked, *scaled_slabs)

    increment = pl.pallas_call(
        functools.partial(total_kernel, member_scale),
        out_shape=bf16((rows, width)),
        in_specs=[VMEM] * outer,
        out_specs=VMEM,
        cost_estimate=cost(10**6, 1 << 18),
        name="total",
    )(*terms)
    return (
        increment.reshape(fields, levels, width),
        gradient.reshape(members, fields, levels, columns),
    )


def solution(mesh):
    placed = (
        P("wide", None, "lev", None),
        P("wide", None, "lev", None),
        P(),
        P(),
        P(),
        P(),
        P(),
        P(None, "lev", "wide"),
    )
    return jax.shard_map(
        body,
        mesh=mesh,
        in_specs=placed,
        out_specs=(P(None, "lev", "wide"), P("wide", None, "lev", None)),
        check_vma=False,
    )
```

time: 54 us -> 52.2 us (0.967)
  blocking collectives: 17.5 us -> 0 us
  waiting for transfers between devices: 2.9 us -> 14.2 us
  starting transfers between devices: 11.9 us -> 18.8 us
  local copies, waits for them, and re-layouts: 5.11 us -> 3.36 us
  other arithmetic: 1.36 us -> 0.78 us
    ppermute x2 -> x14, starting transfers between devices: 0.63 us -> 18.8 us  [the longest x6 10.2 us: along_line(): return lax.ppermute(value, 'wide', pairs)]
    all_to_all x1 -> x0, blocking collectives: 17.5 us -> none  [body(): lax.all_to_all(merged, 'wide', 0, 0, axis_index_groups=planes, tiled=True)]
    ppermute x2 -> x14, waiting for transfers between devices: 0.01 us -> 14.2 us  [the longest x6 9.28 us: in_plane(): return lax.ppermute(value, 'wide', pairs)]
    all_to_all x2 -> x0, starting transfers between devices: 11.3 us -> none  [the longest x1 6.48 us: body(): lax.all_to_all(jnp.broadcast_to(cot_rows, (outer, rows, region_max)), 'wi...]
    all_to_all x2 -> x0, waiting for transfers between devices: 2.89 us -> none  [the longest x1 2.89 us: body(): lax.all_to_all(partial, 'wide', 0, 0, axis_index_groups=lines, tiled=True)]
    slice x2 -> x0, local copies, waits for them, and re-layouts: 1.81 us -> none  [halo_of(): block[:, levels - reach:, :].reshape(halo, columns)]
    concatenate x3 -> x0, other arithmetic: 1.34 us -> none  [the longest x2 1.25 us: halo_of(): return jnp.concatenate([below, above], axis=0)]
    unnamed x9 -> x24, local copies, waits for them, and re-layouts: 2.47 us -> 3.36 us
  transfers between devices with their start and end apart: 4 -> 14, of which waited for: 1 -> 8; matrix products, arithmetic and copies ran while one was open for 5% -> 1% of each run, Pallas kernels for 18% -> 24%
where the time goes in v2:
time: 52.2 us; the launch traced here: 51.8 us
  starting transfers between devices  18.8 us (36%)
  waiting for transfers between devices  14.2 us (27%)
  Pallas kernels  14 us (27%)
  local copies, waits for them, and re-layouts  3.36 us (6%)
  other arithmetic  0.78 us (1%)
  between operations  0.7 us (1%)
    ppermute x6, starting transfers between devices, along_line(): return lax.ppermute(value, 'wide', pairs)  10.2 us
    ppermute x6, waiting for transfers between devices, in_plane(): return lax.ppermute(value, 'wide', pairs)  9.28 us
    ppermute x6, starting transfers between devices, in_plane(): return lax.ppermute(value, 'wide', pairs)  8.57 us
    ppermute x6, waiting for transfers between devices, along_line(): return lax.ppermute(value, 'wide', pairs)  4.92 us
    pallas_call x1, Pallas kernels, body(): pl.pallas_call(functools.partial(forward_kernel, grid), out_shape=[bf16((...  3.53 us
    unnamed x24, local copies, waits for them, and re-layouts  3.36 us
    pallas_call x1, Pallas kernels, body(): pl.pallas_call(backward_kernel, out_shape=bf16((rows, columns)), in_specs...  2.95 us
    pallas_call x1, Pallas kernels, body(): pl.pallas_call(functools.partial(scale_kernel, grid), out_shape=bf16((row...  2.57 us
  transfers between devices with their start and end apart: 14, of which 8 were waited for; matrix products, arithmetic and copies ran while one was open for 1% of the time, Pallas kernels for 24%

profile of v2, /device:TPU:0, one launch (start us, length us, event | category | flops | bytes accessed | tf_op | source)
XLA Modules:
  0.0 51.8 jit_solution(16409562411760336866)
XLA Ops:
  0.6 5.1 %collective-permute-start.9 = (bf16[128,128]{1,0:T(8,128)(2,1)}, bf16[128,128]{1,0:T(8,128)(2,1)S(1)}, u32[]{:S(2)}, u32[]{:S(2)}) collective-permute-start(bf16[128,128]{1,0:T(8,128)(2,1)} %bitcast.14), channel_id=1, source_target_pairs={{0,24},{2,26},{4,28},{6,30},{8,0},{10,2},{12,4},{14,6},{16,8},{18,... | collective-permute-start | bytes 98312 | tf_op jit(solution)/shard_map/ppermute | solution.py:226
  5.8 0.0 collective-permute-start.8
  5.8 1.0 %collective-permute-start.7 = (bf16[128,128]{1,0:T(8,128)(2,1)}, bf16[128,128]{1,0:T(8,128)(2,1)S(1)}, u32[]{:S(2)}, u32[]{:S(2)}) collective-permute-start(bf16[128,128]{1,0:T(8,128)(2,1)} %bitcast.16), channel_id=1, source_target_pairs={{0,8},{2,10},{4,12},{6,14},{8,16},{10,18},{12,20},{14,22},{16,24},... | collective-permute-start | bytes 98312 | tf_op jit(solution)/shard_map/ppermute | solution.py:226
  6.8 0.0 collective-permute-start
  6.8 0.9 %collective-permute-done.9 = bf16[128,128]{1,0:T(8,128)(2,1)S(1)} collective-permute-done((bf16[128,128]{1,0:T(8,128)(2,1)}, bf16[128,128]{1,0:T(8,128)(2,1)S(1)}, u32[]{:S(2)}, u32[]{:S(2)}) %collective-permute-start.9) | collective-permute-done | bytes 32800 | tf_op jit(solution)/shard_map/ppermute | solution.py:226
  7.7 3.1 %collective-permute-done.8 = bf16[128,128]{1,0:T(8,128)(2,1)S(1)} collective-permute-done((bf16[128,128]{1,0:T(8,128)(2,1)}, bf16[128,128]{1,0:T(8,128)(2,1)S(1)}, u32[]{:S(2)}, u32[]{:S(2)}) %collective-permute-start.8) | collective-permute-done | bytes 32800 | tf_op jit(solution)/shard_map/ppermute | solution.py:226
  10.8 0.9 %collective-permute-done.7 = bf16[128,128]{1,0:T(8,128)(2,1)S(1)} collective-permute-done((bf16[128,128]{1,0:T(8,128)(2,1)}, bf16[128,128]{1,0:T(8,128)(2,1)S(1)}, u32[]{:S(2)}, u32[]{:S(2)}) %collective-permute-start.7) | collective-permute-done | bytes 32800 | tf_op jit(solution)/shard_map/ppermute | solution.py:226
  11.7 0.8 %pad_maximum_fusion.refs_0_ = bf16[4,128,128]{2,1,0:T(8,128)(2,1)S(1)} fusion(bf16[1,128,128]{2,1,0:T(8,128)(2,1)S(1)} %bitcast.18, bf16[1,128,128]{2,1,0:T(8,128)(2,1)S(1)} %bitcast.19, bf16[1,128,128]{2,1,0:T(8,128)(2,1)S(1)} %bitcast.20, bf16[1,128,128]{2,1,0:T(8,128)(2,1)} %bitcast.17), kind=kLoop, calls=%fused_computation | loop fusion | flops 196608 | bytes 262144 | tf_op jit(solution)/shard_map/stack | solution.py:242
  12.5 0.0 copy-start
  12.5 1.5 %collective-permute-start.10 = (bf16[4,128,128]{2,1,0:T(8,128)(2,1)S(1)}, bf16[4,128,128]{2,1,0:T(8,128)(2,1)S(1)}, u32[]{:S(2)}, u32[]{:S(2)}) collective-permute-start(bf16[4,128,128]{2,1,0:T(8,128)(2,1)S(1)} %pad_maximum_fusion.refs_0_), channel_id=1, source_target_pairs={{0,2},{2,4},{4,6},{6,0},{8,10},{10,12},{12,14},{14,8},{16,18},{18,... | collective-permute-start | bytes 393224 | tf_op jit(solution)/shard_map/ppermute | solution.py:234
  14.0 1.5 %collective-permute-start.11 = (bf16[4,128,128]{2,1,0:T(8,128)(2,1)S(1)}, bf16[4,128,128]{2,1,0:T(8,128)(2,1)S(1)}, u32[]{:S(2)}, u32[]{:S(2)}) collective-permute-start(bf16[4,128,128]{2,1,0:T(8,128)(2,1)S(1)} %pad_maximum_fusion.refs_0_), channel_id=1, source_target_pairs={{0,4},{2,6},{4,0},{6,2},{8,12},{10,14},{12,8},{14,10},{16,20},{18,... | collective-permute-start | bytes 393224 | tf_op jit(solution)/shard_map/ppermute | solution.py:234
  15.5 1.4 %collective-permute-start.12 = (bf16[4,128,128]{2,1,0:T(8,128)(2,1)S(1)}, bf16[4,128,128]{2,1,0:T(8,128)(2,1)S(1)}, u32[]{:S(2)}, u32[]{:S(2)}) collective-permute-start(bf16[4,128,128]{2,1,0:T(8,128)(2,1)S(1)} %pad_maximum_fusion.refs_0_), channel_id=1, source_target_pairs={{0,6},{2,0},{4,2},{6,4},{8,14},{10,8},{12,10},{14,12},{16,22},{18,... | collective-permute-start | bytes 393224 | tf_op jit(solution)/shard_map/ppermute | solution.py:234
  17.0 1.9 %collective-permute-done.10.refs_1_ = bf16[4,128,128]{2,1,0:T(8,128)(2,1)S(1)} collective-permute-done((bf16[4,128,128]{2,1,0:T(8,128)(2,1)S(1)}, bf16[4,128,128]{2,1,0:T(8,128)(2,1)S(1)}, u32[]{:S(2)}, u32[]{:S(2)}) %collective-permute-start.10) | collective-permute-done | bytes 131104 | tf_op jit(solution)/shard_map/ppermute | solution.py:234
  18.8 0.0 copy-start.1
  18.8 1.3 %collective-permute-done.11.refs_2_ = bf16[4,128,128]{2,1,0:T(8,128)(2,1)S(1)} collective-permute-done((bf16[4,128,128]{2,1,0:T(8,128)(2,1)S(1)}, bf16[4,128,128]{2,1,0:T(8,128)(2,1)S(1)}, u32[]{:S(2)}, u32[]{:S(2)}) %collective-permute-start.11) | collective-permute-done | bytes 131104 | tf_op jit(solution)/shard_map/ppermute | solution.py:234
  20.1 0.0 copy-start.2
  20.1 0.4 collective-permute-done.12.refs_3_
  20.5 0.0 copy-start.3
  20.5 0.0 copy-done
  20.5 0.0 copy-done.1
  20.5 0.2 copy-done.2
  20.7 0.4 copy-done.3
  21.2 2.6 %scale.1.refs_0_ = bf16[128,1024]{1,0:T(8,128)(2,1)} custom-call(s32[16]{0:T(128)} %sizes_ref.3, s32[16]{0:T(128)} %owner_ref.3, bf16[128,1024]{1,0:T(8,128)(2,1)} %bitcast.11, bf16[4,128,128]{2,1,0:T(8,128)(2,1)} %copy-done, bf16[4,128,128]{2,1,0:T(8,128)(2,1)} %copy-done.1, bf16[4,128,128]{2,1,0:T(8,128)(2,1)} %copy-done.2, bf16[4,128,128]{2,1,0:T(8,128)(2,1)} %copy-done.3), custom_call_target="tpu_custom_call" | custom-call | flops 10000000 | bytes 1048576 | tf_op jit(solution)/shard_map/scale/pallas_call | solution.py:280
  23.7 0.0 collective-permute-start.13
  23.7 1.7 %weights.1 = (bf16[2,256,128]{2,1,0:T(8,128)(2,1)}, bf16[2,128,256]{2,1,0:T(8,128)(2,1)}) custom-call(f32[9,64]{1,0:T(8,128)} %bitcast.21), custom_call_target="tpu_custom_call" | custom-call | flops 1000000 | bytes 100000 | tf_op jit(solution)/shard_map/weights/pallas_call | solution.py:245
  25.4 0.0 collective-permute-done.refs_1_
  25.4 0.0 copy-start.11
  25.5 0.7 %copy-done.11 = bf16[128,1024]{1,0:T(8,128)(2,1)} copy-done((bf16[128,1024]{1,0:T(8,128)(2,1)}, bf16[128,1024]{1,0:T(8,128)(2,1)S(1)}, u32[]{:S(2)}) %copy-start.11) | copy-done | bytes 262168
  26.2 3.5 %forward.1 = (bf16[4,128,128]{2,1,0:T(8,128)(2,1)}, bf16[4,128,128]{2,1,0:T(8,128)(2,1)}, bf16[4,128,128]{2,1,0:T(8,128)(2,1)}, bf16[4,128,128]{2,1,0:T(8,128)(2,1)}) custom-call(s32[8,8]{1,0:T(8,128)} %pattern_ref.3, s32[16]{0:T(128)} %sizes_ref.3, s32[16]{0:T(128)} %owner_ref.3, bf16[2,256,128]{2,1,0:T(8,128)(2,1)} %get-tuple-element.12.down_ref, ...), custom_call_target="tpu_custom_call" | custom-call | flops 1000000000 | bytes 2097152 | tf_op jit(solution)/shard_map/forward/pallas_call | solution.py:255
  29.7 1.4 %collective-permute-start.1 = (bf16[4,128,128]{2,1,0:T(8,128)(2,1)}, bf16[4,128,128]{2,1,0:T(8,128)(2,1)S(1)}, u32[]{:S(2)}, u32[]{:S(2)}) collective-permute-start(bf16[4,128,128]{2,1,0:T(8,128)(2,1)} %get-tuple-element.14), channel_id=1, source_target_pairs={{0,2},{2,4},{4,6},{6,0},{8,10},{10,12},{12,14},{14,8},{16,18},{18,... | collective-permute-start | bytes 393224 | tf_op jit(solution)/shard_map/ppermute | solution.py:234
  31.1 1.5 %collective-permute-start.2 = (bf16[4,128,128]{2,1,0:T(8,128)(2,1)}, bf16[4,128,128]{2,1,0:T(8,128)(2,1)S(1)}, u32[]{:S(2)}, u32[]{:S(2)}) collective-permute-start(bf16[4,128,128]{2,1,0:T(8,128)(2,1)} %get-tuple-element.15), channel_id=1, source_target_pairs={{0,4},{2,6},{4,0},{6,2},{8,12},{10,14},{12,8},{14,10},{16,20},{18,... | collective-permute-start | bytes 393224 | tf_op jit(solution)/shard_map/ppermute | solution.py:234
  32.6 1.2 %collective-permute-start.3 = (bf16[4,128,128]{2,1,0:T(8,128)(2,1)}, bf16[4,128,128]{2,1,0:T(8,128)(2,1)S(1)}, u32[]{:S(2)}, u32[]{:S(2)}) collective-permute-start(bf16[4,128,128]{2,1,0:T(8,128)(2,1)} %get-tuple-element.16), channel_id=1, source_target_pairs={{0,6},{2,0},{4,2},{6,4},{8,14},{10,8},{12,10},{14,12},{16,22},{18,... | collective-permute-start | bytes 393224 | tf_op jit(solution)/shard_map/ppermute | solution.py:234
  33.8 3.4 %collective-permute-done.1.refs_1_ = bf16[4,128,128]{2,1,0:T(8,128)(2,1)S(1)} collective-permute-done((bf16[4,128,128]{2,1,0:T(8,128)(2,1)}, bf16[4,128,128]{2,1,0:T(8,128)(2,1)S(1)}, u32[]{:S(2)}, u32[]{:S(2)}) %collective-permute-start.1) | collective-permute-done | bytes 131104 | tf_op jit(solution)/shard_map/ppermute | solution.py:234
  37.2 0.0 copy-start.4
  37.2 2.3 %collective-permute-done.2.refs_2_ = bf16[4,128,128]{2,1,0:T(8,128)(2,1)S(1)} collective-permute-done((bf16[4,128,128]{2,1,0:T(8,128)(2,1)}, bf16[4,128,128]{2,1,0:T(8,128)(2,1)S(1)}, u32[]{:S(2)}, u32[]{:S(2)}) %collective-permute-start.2) | collective-permute-done | bytes 131104 | tf_op jit(solution)/shard_map/ppermute | solution.py:234
  39.5 0.0 copy-start.5
  39.5 0.0 collective-permute-done.3.refs_3_
  39.5 0.0 copy-start.6
  39.5 0.0 copy-done.4
  39.5 0.6 %copy-done.5 = bf16[4,128,128]{2,1,0:T(8,128)(2,1)} copy-done((bf16[4,128,128]{2,1,0:T(8,128)(2,1)}, bf16[4,128,128]{2,1,0:T(8,128)(2,1)S(1)}, u32[]{:S(2)}) %copy-start.5) | copy-done | bytes 131096
  40.2 0.0 copy-done.6
  40.2 1.8 %partial.1 = (bf16[128,128]{1,0:T(8,128)(2,1)}, bf16[128,128]{1,0:T(8,128)(2,1)}, bf16[128,128]{1,0:T(8,128)(2,1)}, bf16[128,128]{1,0:T(8,128)(2,1)}) custom-call(bf16[4,128,128]{2,1,0:T(8,128)(2,1)} %get-tuple-element.13.refs_0_, bf16[4,128,128]{2,1,0:T(8,128)(2,1)} %copy-done.4, bf16[4,128,128]{2,1,0:T(8,128)(2,1)} %copy-done.5, bf16[4,128,128]{2,1,0:T(8,128)(2,1)} %copy-done.6), custom_call_target="tpu_custom_call" | custom-call | flops 1000000 | bytes 1048576 | tf_op jit(solution)/shard_map/partial/pallas_call | solution.py:270
  42.0 0.0 collective-permute-start.4
  42.0 1.2 %collective-permute-start.5 = (bf16[128,128]{1,0:T(8,128)(2,1)}, bf16[128,128]{1,0:T(8,128)(2,1)S(1)}, u32[]{:S(2)}, u32[]{:S(2)}) collective-permute-start(bf16[128,128]{1,0:T(8,128)(2,1)} %get-tuple-element.19), channel_id=1, source_target_pairs={{0,16},{2,18},{4,20},{6,22},{8,24},{10,26},{12,28},{14,30},{16,0},... | collective-permute-start | bytes 98312 | tf_op jit(solution)/shard_map/ppermute | solution.py:226
  43.1 2.9 %collective-permute-start.6 = (bf16[128,128]{1,0:T(8,128)(2,1)}, bf16[128,128]{1,0:T(8,128)(2,1)S(1)}, u32[]{:S(2)}, u32[]{:S(2)}) collective-permute-start(bf16[128,128]{1,0:T(8,128)(2,1)} %get-tuple-element.20), channel_id=1, source_target_pairs={{0,24},{2,26},{4,28},{6,30},{8,0},{10,2},{12,4},{14,6},{16,8},{18,... | collective-permute-start | bytes 98312 | tf_op jit(solution)/shard_map/ppermute | solution.py:226
  46.0 0.0 collective-permute-done.13.refs_1_
  46.0 0.0 copy-start.10
  46.0 0.7 %copy-done.10 = bf16[128,1024]{1,0:T(8,128)(2,1)} copy-done((bf16[128,1024]{1,0:T(8,128)(2,1)}, bf16[128,1024]{1,0:T(8,128)(2,1)S(1)}, u32[]{:S(2)}) %copy-start.10) | copy-done | bytes 262168
  46.7 3.0 %backward.1 = bf16[128,1024]{1,0:T(8,128)(2,1)} custom-call(s32[8,8]{1,0:T(8,128)} %pattern_ref.3, bf16[2,128,256]{2,1,0:T(8,128)(2,1)} %get-tuple-element.21.up_ref, bf16[1024,128]{1,0:T(8,128)(2,1)} %bitcast.25, bf16[128,1024]{1,0:T(8,128)(2,1)} %scale.1.refs_0_, bf16[128,1024]{1,0:T(8,128)(2,1)} %copy-done.10), custom_call_target="tpu_custom_call" | custom-call | flops 1000000000 | bytes 1048576 | tf_op jit(solution)/shard_map/backward/pallas_call | solution.py:293
  49.7 0.0 collective-permute-done.4.refs_1_
  49.7 0.0 copy-start.7
  49.7 0.0 collective-permute-done.5.refs_2_
  49.7 0.0 copy-start.8
  49.7 0.0 collective-permute-done.6.refs_3_
  49.7 0.0 copy-start.9
  49.7 0.6 %copy-done.7 = bf16[128,128]{1,0:T(8,128)(2,1)} copy-done((bf16[128,128]{1,0:T(8,128)(2,1)}, bf16[128,128]{1,0:T(8,128)(2,1)S(1)}, u32[]{:S(2)}) %copy-start.7) | copy-done | bytes 32792
  50.3 0.0 copy-done.8
  50.3 0.0 copy-done.9
  50.3 1.4 %total.1 = bf16[128,128]{1,0:T(8,128)(2,1)} custom-call(bf16[128,128]{1,0:T(8,128)(2,1)} %get-tuple-element.17.refs_0_, bf16[128,128]{1,0:T(8,128)(2,1)} %copy-done.7, bf16[128,128]{1,0:T(8,128)(2,1)} %copy-done.8, bf16[128,128]{1,0:T(8,128)(2,1)} %copy-done.9), custom_call_target="tpu_custom_call" | custom-call | flops 1000000 | bytes 262144 | tf_op jit(solution)/shard_map/total/pallas_call | solution.py:306
Async XLA Ops:
  0.6 7.0 %collective-permute-start.9 = (bf16[128,128]{1,0:T(8,128)(2,1)}, bf16[128,128]{1,0:T(8,128)(2,1)S(1)}, u32[]{:S(2)}, u32[]{:S(2)}) collective-permute-start(bf16[128,128]{1,0:T(8,128)(2,1)} %bitcast.14), channel_id=1, source_target_pairs={{0,24},{2,26},{4,28},{6,30},{8,0},{10,2},{12,4},{14,6},{16,8},{18,... | collective-permute-start | bytes 98312 | tf_op jit(solution)/shard_map/ppermute | solution.py:226
  5.8 5.0 %collective-permute-start.8 = (bf16[128,128]{1,0:T(8,128)(2,1)}, bf16[128,128]{1,0:T(8,128)(2,1)S(1)}, u32[]{:S(2)}, u32[]{:S(2)}) collective-permute-start(bf16[128,128]{1,0:T(8,128)(2,1)} %bitcast.15), channel_id=1, source_target_pairs={{0,16},{2,18},{4,20},{6,22},{8,24},{10,26},{12,28},{14,30},{16,0},... | collective-permute-start | bytes 98312 | tf_op jit(solution)/shard_map/ppermute | solution.py:226
  5.8 5.9 %collective-permute-start.7 = (bf16[128,128]{1,0:T(8,128)(2,1)}, bf16[128,128]{1,0:T(8,128)(2,1)S(1)}, u32[]{:S(2)}, u32[]{:S(2)}) collective-permute-start(bf16[128,128]{1,0:T(8,128)(2,1)} %bitcast.16), channel_id=1, source_target_pairs={{0,8},{2,10},{4,12},{6,14},{8,16},{10,18},{12,20},{14,22},{16,24},... | collective-permute-start | bytes 98312 | tf_op jit(solution)/shard_map/ppermute | solution.py:226
  6.8 18.7 %collective-permute-start = (bf16[128,1024]{1,0:T(8,128)(2,1)}, bf16[128,1024]{1,0:T(8,128)(2,1)S(1)}, u32[]{:S(2)}, u32[]{:S(2)}) collective-permute-start(bf16[128,1024]{1,0:T(8,128)(2,1)} %bitcast.22), channel_id=1, source_target_pairs={{0,1},{1,0},{2,3},{3,2},{4,5},{5,4},{6,7},{7,6},{8,9},{9,8},{10,11... | collective-permute-start | bytes 786440 | tf_op jit(solution)/shard_map/ppermute | solution.py:21
  12.5 8.0 %copy-start = (bf16[4,128,128]{2,1,0:T(8,128)(2,1)}, bf16[4,128,128]{2,1,0:T(8,128)(2,1)S(1)}, u32[]{:S(2)}) copy-start(bf16[4,128,128]{2,1,0:T(8,128)(2,1)S(1)} %pad_maximum_fusion.refs_0_) | copy-start | bytes 393220
  12.5 6.4 %collective-permute-start.10 = (bf16[4,128,128]{2,1,0:T(8,128)(2,1)S(1)}, bf16[4,128,128]{2,1,0:T(8,128)(2,1)S(1)}, u32[]{:S(2)}, u32[]{:S(2)}) collective-permute-start(bf16[4,128,128]{2,1,0:T(8,128)(2,1)S(1)} %pad_maximum_fusion.refs_0_), channel_id=1, source_target_pairs={{0,2},{2,4},{4,6},{6,0},{8,10},{10,12},{12,14},{14,8},{16,18},{18,... | collective-permute-start | bytes 393224 | tf_op jit(solution)/shard_map/ppermute | solution.py:234
  14.0 6.1 %collective-permute-start.11 = (bf16[4,128,128]{2,1,0:T(8,128)(2,1)S(1)}, bf16[4,128,128]{2,1,0:T(8,128)(2,1)S(1)}, u32[]{:S(2)}, u32[]{:S(2)}) collective-permute-start(bf16[4,128,128]{2,1,0:T(8,128)(2,1)S(1)} %pad_maximum_fusion.refs_0_), channel_id=1, source_target_pairs={{0,4},{2,6},{4,0},{6,2},{8,12},{10,14},{12,8},{14,10},{16,20},{18,... | collective-permute-start | bytes 393224 | tf_op jit(solution)/shard_map/ppermute | solution.py:234
  15.5 5.0 %collective-permute-start.12 = (bf16[4,128,128]{2,1,0:T(8,128)(2,1)S(1)}, bf16[4,128,128]{2,1,0:T(8,128)(2,1)S(1)}, u32[]{:S(2)}, u32[]{:S(2)}) collective-permute-start(bf16[4,128,128]{2,1,0:T(8,128)(2,1)S(1)} %pad_maximum_fusion.refs_0_), channel_id=1, source_target_pairs={{0,6},{2,0},{4,2},{6,4},{8,14},{10,8},{12,10},{14,12},{16,22},{18,... | collective-permute-start | bytes 393224 | tf_op jit(solution)/shard_map/ppermute | solution.py:234
  18.8 1.7 %copy-start.1 = (bf16[4,128,128]{2,1,0:T(8,128)(2,1)}, bf16[4,128,128]{2,1,0:T(8,128)(2,1)S(1)}, u32[]{:S(2)}) copy-start(bf16[4,128,128]{2,1,0:T(8,128)(2,1)S(1)} %collective-permute-done.10.refs_1_) | copy-start | bytes 393220
  20.1 0.7 %copy-start.2 = (bf16[4,128,128]{2,1,0:T(8,128)(2,1)}, bf16[4,128,128]{2,1,0:T(8,128)(2,1)S(1)}, u32[]{:S(2)}) copy-start(bf16[4,128,128]{2,1,0:T(8,128)(2,1)S(1)} %collective-permute-done.11.refs_2_) | copy-start | bytes 393220
  20.5 0.7 %copy-start.3 = (bf16[4,128,128]{2,1,0:T(8,128)(2,1)}, bf16[4,128,128]{2,1,0:T(8,128)(2,1)S(1)}, u32[]{:S(2)}) copy-start(bf16[4,128,128]{2,1,0:T(8,128)(2,1)S(1)} %collective-permute-done.12.refs_3_) | copy-start | bytes 393220
  23.7 22.3 %collective-permute-start.13 = (bf16[128,1024]{1,0:T(8,128)(2,1)}, bf16[128,1024]{1,0:T(8,128)(2,1)S(1)}, u32[]{:S(2)}, u32[]{:S(2)}) collective-permute-start(bf16[128,1024]{1,0:T(8,128)(2,1)} %scale.1.refs_0_), channel_id=1, source_target_pairs={{0,1},{1,0},{2,3},{3,2},{4,5},{5,4},{6,7},{7,6},{8,9},{9,8},{10,11... | collective-permute-start | bytes 786440 | tf_op jit(solution)/shard_map/ppermute | solution.py:21
  25.4 0.7 %copy-start.11 = (bf16[128,1024]{1,0:T(8,128)(2,1)}, bf16[128,1024]{1,0:T(8,128)(2,1)S(1)}, u32[]{:S(2)}) copy-start(bf16[128,1024]{1,0:T(8,128)(2,1)S(1)} %collective-permute-done.refs_1_) | copy-start | bytes 786436
  29.7 7.5 %collective-permute-start.1 = (bf16[4,128,128]{2,1,0:T(8,128)(2,1)}, bf16[4,128,128]{2,1,0:T(8,128)(2,1)S(1)}, u32[]{:S(2)}, u32[]{:S(2)}) collective-permute-start(bf16[4,128,128]{2,1,0:T(8,128)(2,1)} %get-tuple-element.14), channel_id=1, source_target_pairs={{0,2},{2,4},{4,6},{6,0},{8,10},{10,12},{12,14},{14,8},{16,18},{18,... | collective-permute-start | bytes 393224 | tf_op jit(solution)/shard_map/ppermute | solution.py:234
  31.1 8.4 %collective-permute-start.2 = (bf16[4,128,128]{2,1,0:T(8,128)(2,1)}, bf16[4,128,128]{2,1,0:T(8,128)(2,1)S(1)}, u32[]{:S(2)}, u32[]{:S(2)}) collective-permute-start(bf16[4,128,128]{2,1,0:T(8,128)(2,1)} %get-tuple-element.15), channel_id=1, source_target_pairs={{0,4},{2,6},{4,0},{6,2},{8,12},{10,14},{12,8},{14,10},{16,20},{18,... | collective-permute-start | bytes 393224 | tf_op jit(solution)/shard_map/ppermute | solution.py:234
  32.6 6.9 %collective-permute-start.3 = (bf16[4,128,128]{2,1,0:T(8,128)(2,1)}, bf16[4,128,128]{2,1,0:T(8,128)(2,1)S(1)}, u32[]{:S(2)}, u32[]{:S(2)}) collective-permute-start(bf16[4,128,128]{2,1,0:T(8,128)(2,1)} %get-tuple-element.16), channel_id=1, source_target_pairs={{0,6},{2,0},{4,2},{6,4},{8,14},{10,8},{12,10},{14,12},{16,22},{18,... | collective-permute-start | bytes 393224 | tf_op jit(solution)/shard_map/ppermute | solution.py:234
  37.2 2.3 %copy-start.4 = (bf16[4,128,128]{2,1,0:T(8,128)(2,1)}, bf16[4,128,128]{2,1,0:T(8,128)(2,1)S(1)}, u32[]{:S(2)}) copy-start(bf16[4,128,128]{2,1,0:T(8,128)(2,1)S(1)} %collective-permute-done.1.refs_1_) | copy-start | bytes 393220
  39.5 0.7 %copy-start.5 = (bf16[4,128,128]{2,1,0:T(8,128)(2,1)}, bf16[4,128,128]{2,1,0:T(8,128)(2,1)S(1)}, u32[]{:S(2)}) copy-start(bf16[4,128,128]{2,1,0:T(8,128)(2,1)S(1)} %collective-permute-done.2.refs_2_) | copy-start | bytes 393220
  39.5 0.7 %copy-start.6 = (bf16[4,128,128]{2,1,0:T(8,128)(2,1)}, bf16[4,128,128]{2,1,0:T(8,128)(2,1)S(1)}, u32[]{:S(2)}) copy-start(bf16[4,128,128]{2,1,0:T(8,128)(2,1)S(1)} %collective-permute-done.3.refs_3_) | copy-start | bytes 393220
  42.0 7.7 %collective-permute-start.4 = (bf16[128,128]{1,0:T(8,128)(2,1)}, bf16[128,128]{1,0:T(8,128)(2,1)S(1)}, u32[]{:S(2)}, u32[]{:S(2)}) collective-permute-start(bf16[128,128]{1,0:T(8,128)(2,1)} %get-tuple-element.18), channel_id=1, source_target_pairs={{0,8},{2,10},{4,12},{6,14},{8,16},{10,18},{12,20},{14,22},{16,24},... | collective-permute-start | bytes 98312 | tf_op jit(solution)/shard_map/ppermute | solution.py:226
  42.0 7.7 %collective-permute-start.5 = (bf16[128,128]{1,0:T(8,128)(2,1)}, bf16[128,128]{1,0:T(8,128)(2,1)S(1)}, u32[]{:S(2)}, u32[]{:S(2)}) collective-permute-start(bf16[128,128]{1,0:T(8,128)(2,1)} %get-tuple-element.19), channel_id=1, source_target_pairs={{0,16},{2,18},{4,20},{6,22},{8,24},{10,26},{12,28},{14,30},{16,0},... | collective-permute-start | bytes 98312 | tf_op jit(solution)/shard_map/ppermute | solution.py:226
  43.1 6.6 %collective-permute-start.6 = (bf16[128,128]{1,0:T(8,128)(2,1)}, bf16[128,128]{1,0:T(8,128)(2,1)S(1)}, u32[]{:S(2)}, u32[]{:S(2)}) collective-permute-start(bf16[128,128]{1,0:T(8,128)(2,1)} %get-tuple-element.20), channel_id=1, source_target_pairs={{0,24},{2,26},{4,28},{6,30},{8,0},{10,2},{12,4},{14,6},{16,8},{18,... | collective-permute-start | bytes 98312 | tf_op jit(solution)/shard_map/ppermute | solution.py:226
  46.0 0.7 %copy-start.10 = (bf16[128,1024]{1,0:T(8,128)(2,1)}, bf16[128,1024]{1,0:T(8,128)(2,1)S(1)}, u32[]{:S(2)}) copy-start(bf16[128,1024]{1,0:T(8,128)(2,1)S(1)} %collective-permute-done.13.refs_1_) | copy-start | bytes 786436
  49.7 0.6 %copy-start.7 = (bf16[128,128]{1,0:T(8,128)(2,1)}, bf16[128,128]{1,0:T(8,128)(2,1)S(1)}, u32[]{:S(2)}) copy-start(bf16[128,128]{1,0:T(8,128)(2,1)S(1)} %collective-permute-done.4.refs_1_) | copy-start | bytes 98308
  49.7 0.6 %copy-start.8 = (bf16[128,128]{1,0:T(8,128)(2,1)}, bf16[128,128]{1,0:T(8,128)(2,1)S(1)}, u32[]{:S(2)}) copy-start(bf16[128,128]{1,0:T(8,128)(2,1)S(1)} %collective-permute-done.5.refs_2_) | copy-start | bytes 98308
  49.7 0.6 %copy-start.9 = (bf16[128,128]{1,0:T(8,128)(2,1)}, bf16[128,128]{1,0:T(8,128)(2,1)S(1)}, u32[]{:S(2)}) copy-start(bf16[128,128]{1,0:T(8,128)(2,1)S(1)} %collective-permute-done.6.refs_3_) | copy-start | bytes 98308

commit v3 on v2

--- a/solution.py
+++ b/solution.py
@@ -85,15 +85,16 @@
     lax.fori_loop(0, sizes_ref.shape[0], step, jnp.int32(0), unroll=4)
 
 
-def forward_kernel(grid, pattern_ref, sizes_ref, owner_ref, down_ref, ens_ref, htile_ref, *refs):
+def forward_kernel(grid, pattern_ref, sizes_ref, owner_ref, both_ref, down_ref, htile_ref, *refs):
     outer, inner = grid
     out_refs = refs[-inner - 3 : -3]
     slab_refs = refs[: -inner - 3]
     mixed, product, placed = refs[-3:]
     blocks, slots = pattern_ref.shape
-    rows = ens_ref.shape[0]
+    rows = both_ref.shape[0] // 2
+    ens_ref = both_ref.at[rows:]
     width = htile_ref.shape[1]
-    extended = jnp.concatenate([ref[...] for ref in slab_refs], axis=0)
+    extended = jnp.concatenate([both_ref[:rows]] + [ref[...] for ref in slab_refs], axis=0)
     dims = (((0,), (0,)), ((), ()))
     summed = lax.dot_general(down_ref[0], extended, dims, preferred_element_type=jnp.float32)
     summed = summed + lax.dot_general(
@@ -195,6 +196,9 @@
     for part in refs[1:-1]:
         total = total + part[...].astype(jnp.float32)
     refs[-1][...] = (total * scale).astype(jnp.bfloat16)
+
+
+PARAMS = pltpu.CompilerParams(vmem_limit_bytes=8 << 20)
 
 
 def cost(flops, moved):
@@ -242,12 +246,14 @@
     cot_line = jnp.stack([cot_rows] + [along_line(cot_rows, i) for i in range(1, outer)])
     cot_parts = [cot_line] + [in_plane(cot_line, i) for i in range(1, inner)]
 
+    both = lax.concatenate([alpha_rows, ens_rows], 0)
     down, up = pl.pallas_call(
         functools.partial(weight_kernel, fields, slabs),
         out_shape=(bf16((2, span, rows)), bf16((2, rows, span))),
         in_specs=[VMEM],
         out_specs=(VMEM, VMEM),
         scratch_shapes=[pltpu.VMEM((2 * 8, LANES), jnp.float32)],
+        compiler_params=PARAMS,
         cost_estimate=cost(10**6, 10**5),
         name="weights",
     )(vloc.T)
@@ -255,16 +261,17 @@
     sent = pl.pallas_call(
         functools.partial(forward_kernel, grid),
         out_shape=[bf16((outer, rows, width))] * inner,
-        in_specs=[SMEM] * 3 + [VMEM] * (3 + len(alpha_slabs)),
+        in_specs=[SMEM] * 3 + [VMEM] * (2 + len(alpha_slabs)),
         out_specs=[VMEM] * inner,
         scratch_shapes=[
             pltpu.VMEM((blocks, rows, width), jnp.bfloat16),
             pltpu.VMEM((blocks + 1, rows, width), jnp.float32),
             pltpu.VMEM((inner, outer, rows, width), jnp.bfloat16),
         ],
+        compiler_params=PARAMS,
         cost_estimate=cost(10**9, 2 << 20),
         name="forward",
-    )(pattern, region_sizes, owner, down, ens_rows, stacked, *alpha_slabs)
+    )(pattern, region_sizes, owner, both, down, stacked, *alpha_slabs[1:])
 
     arrived = [sent[0]] + [in_plane(sent[i], i) for i in range(1, inner)]
     partial = pl.pallas_call(
@@ -272,6 +279,7 @@
         out_shape=[bf16((rows, width))] * outer,
         in_specs=[VMEM] * inner,
         out_specs=[VMEM] * outer,
+        compiler_params=PARAMS,
         cost_estimate=cost(10**6, 1 << 20),
         name="partial",
     )(*arrived)
@@ -286,6 +294,7 @@
             pltpu.VMEM((inner, outer, rows, width), jnp.bfloat16),
             pltpu.VMEM((blocks + 1, rows, width), jnp.float32),
         ],
+        compiler_params=PARAMS,
         cost_estimate=cost(10**7, 1 << 20),
         name="scale",
     )(region_sizes, owner, ens_rows, *cot_parts)
@@ -299,6 +308,7 @@
             pltpu.VMEM((blocks, rows, width), jnp.bfloat16),
             pltpu.VMEM((blocks, rows, width), jnp.float32),
         ],
+        compiler_params=PARAMS,
         cost_estimate=cost(10**9, 1 << 20),
         name="backward",
     )(pattern, up, stacked, *scaled_slabs)
@@ -308,6 +318,7 @@
         out_shape=bf16((rows, width)),
         in_specs=[VMEM] * outer,
         out_specs=VMEM,
+        compiler_params=PARAMS,
         cost_estimate=cost(10**6, 1 << 18),
         name="total",
     )(*terms)

time: 52.2 us -> 41.9 us (0.80)
  Pallas kernels: 14 us -> 6.75 us
  local copies, waits for them, and re-layouts: 3.36 us -> 0.94 us
  waiting for transfers between devices: 14.2 us -> 13.5 us
    unnamed x24 -> x14, local copies, waits for them, and re-layouts: 3.36 us -> 0.94 us
    pallas_call x1, Pallas kernels: 1.76 us -> 0.07 us  [body(): pl.pallas_call(partial_kernel, out_shape=[bf16((rows, width))] * outer, i...]
    pallas_call x1, Pallas kernels: 3.53 us -> 2.12 us  [body(): pl.pallas_call(functools.partial(forward_kernel, grid), out_shape=[bf16((...]
    pallas_call x1, Pallas kernels: 1.71 us -> 0.32 us  [body(): pl.pallas_call(functools.partial(weight_kernel, fields, slabs), out_shape...]
    pallas_call x1, Pallas kernels: 2.57 us -> 1.23 us  [body(): pl.pallas_call(functools.partial(scale_kernel, grid), out_shape=bf16((row...]
    pallas_call x1, Pallas kernels: 1.44 us -> 0.64 us  [body(): pl.pallas_call(functools.partial(total_kernel, member_scale), out_shape=b...]
    ppermute x6, waiting for transfers between devices: 9.28 us -> 8.53 us  [in_plane(): return lax.ppermute(value, 'wide', pairs)]
    pallas_call x1, Pallas kernels: 2.95 us -> 2.38 us  [body(): pl.pallas_call(backward_kernel, out_shape=bf16((rows, columns)), in_specs...]
  transfers between devices with their start and end apart: 14 -> 14, of which waited for: 8 -> 8; matrix products, arithmetic and copies ran while one was open for 1% -> 2% of each run, Pallas kernels for 24% -> 15%
where the time goes in v3:
time: 41.9 us; the launch traced here: 41.6 us
  starting transfers between devices  18.9 us (45%)
  waiting for transfers between devices  13.5 us (32%)
  Pallas kernels  6.75 us (16%)
  local copies, waits for them, and re-layouts  0.94 us (2%)
  other arithmetic  0.81 us (2%)
  between operations  0.77 us (2%)
    ppermute x6, starting transfers between devices, along_line(): return lax.ppermute(value, 'wide', pairs)  10.2 us
    ppermute x6, starting transfers between devices, in_plane(): return lax.ppermute(value, 'wide', pairs)  8.6 us
    ppermute x6, waiting for transfers between devices, in_plane(): return lax.ppermute(value, 'wide', pairs)  8.53 us
    ppermute x6, waiting for transfers between devices, along_line(): return lax.ppermute(value, 'wide', pairs)  4.92 us
    pallas_call x1, Pallas kernels, body(): pl.pallas_call(backward_kernel, out_shape=bf16((rows, columns)), in_specs...  2.38 us
    pallas_call x1, Pallas kernels, body(): pl.pallas_call(functools.partial(forward_kernel, grid), out_shape=[bf16((...  2.12 us
    pallas_call x1, Pallas kernels, body(): pl.pallas_call(functools.partial(scale_kernel, grid), out_shape=bf16((row...  1.23 us
    unnamed x14, local copies, waits for them, and re-layouts  0.94 us
  transfers between devices with their start and end apart: 14, of which 8 were waited for; matrix products, arithmetic and copies ran while one was open for 2% of the time, Pallas kernels for 15%

profile of v3, /device:TPU:0, one launch (start us, length us, event | category | flops | bytes accessed | tf_op | source)
XLA Modules:
  0.0 41.6 jit_solution(17996674503248647106)
XLA Ops:
  0.6 0.0 copy-start
  0.6 5.1 %collective-permute-start.9 = (bf16[128,128]{1,0:T(8,128)(2,1)}, bf16[128,128]{1,0:T(8,128)(2,1)S(1)}, u32[]{:S(2)}, u32[]{:S(2)}) collective-permute-start(bf16[128,128]{1,0:T(8,128)(2,1)} %bitcast.19), channel_id=1, source_target_pairs={{0,24},{2,26},{4,28},{6,30},{8,0},{10,2},{12,4},{14,6},{16,8},{18,... | collective-permute-start | bytes 98312 | tf_op jit(solution)/shard_map/ppermute | solution.py:230
  5.8 0.0 collective-permute-start.8
  5.8 1.0 %collective-permute-start.7 = (bf16[128,128]{1,0:T(8,128)(2,1)}, bf16[128,128]{1,0:T(8,128)(2,1)S(1)}, u32[]{:S(2)}, u32[]{:S(2)}) collective-permute-start(bf16[128,128]{1,0:T(8,128)(2,1)} %bitcast.21), channel_id=1, source_target_pairs={{0,8},{2,10},{4,12},{6,14},{8,16},{10,18},{12,20},{14,22},{16,24},... | collective-permute-start | bytes 98312 | tf_op jit(solution)/shard_map/ppermute | solution.py:230
  6.8 0.0 collective-permute-start
  6.8 0.9 %collective-permute-done.9 = bf16[128,128]{1,0:T(8,128)(2,1)S(1)} collective-permute-done((bf16[128,128]{1,0:T(8,128)(2,1)}, bf16[128,128]{1,0:T(8,128)(2,1)S(1)}, u32[]{:S(2)}, u32[]{:S(2)}) %collective-permute-start.9) | collective-permute-done | bytes 32800 | tf_op jit(solution)/shard_map/ppermute | solution.py:230
  7.7 3.1 %collective-permute-done.8 = bf16[128,128]{1,0:T(8,128)(2,1)S(1)} collective-permute-done((bf16[128,128]{1,0:T(8,128)(2,1)}, bf16[128,128]{1,0:T(8,128)(2,1)S(1)}, u32[]{:S(2)}, u32[]{:S(2)}) %collective-permute-start.8) | collective-permute-done | bytes 32800 | tf_op jit(solution)/shard_map/ppermute | solution.py:230
  10.8 0.9 %collective-permute-done.7 = bf16[128,128]{1,0:T(8,128)(2,1)S(1)} collective-permute-done((bf16[128,128]{1,0:T(8,128)(2,1)}, bf16[128,128]{1,0:T(8,128)(2,1)S(1)}, u32[]{:S(2)}, u32[]{:S(2)}) %collective-permute-start.7) | collective-permute-done | bytes 32800 | tf_op jit(solution)/shard_map/ppermute | solution.py:230
  11.7 0.8 %pad_maximum_fusion.1.refs_0_ = bf16[4,128,128]{2,1,0:T(8,128)(2,1)S(1)} fusion(bf16[1,128,128]{2,1,0:T(8,128)(2,1)S(1)} %bitcast.23, bf16[1,128,128]{2,1,0:T(8,128)(2,1)S(1)} %bitcast.24, bf16[1,128,128]{2,1,0:T(8,128)(2,1)S(1)} %bitcast.25, bf16[1,128,128]{2,1,0:T(8,128)(2,1)} %bitcast.22), kind=kLoop, calls=%fused_computation.1 | loop fusion | flops 196608 | bytes 262144 | tf_op jit(solution)/shard_map/stack | solution.py:246
  12.5 0.0 copy-start.2
  12.5 0.0 copy-start.3
  12.5 1.5 %collective-permute-start.10 = (bf16[4,128,128]{2,1,0:T(8,128)(2,1)S(1)}, bf16[4,128,128]{2,1,0:T(8,128)(2,1)S(1)}, u32[]{:S(2)}, u32[]{:S(2)}) collective-permute-start(bf16[4,128,128]{2,1,0:T(8,128)(2,1)S(1)} %pad_maximum_fusion.1.refs_0_), channel_id=1, source_target_pairs={{0,2},{2,4},{4,6},{6,0},{8,10},{10,12},{12,14},{14,8},{16,18},{18,... | collective-permute-start | bytes 393224 | tf_op jit(solution)/shard_map/ppermute | solution.py:238
  14.0 1.5 %collective-permute-start.11 = (bf16[4,128,128]{2,1,0:T(8,128)(2,1)S(1)}, bf16[4,128,128]{2,1,0:T(8,128)(2,1)S(1)}, u32[]{:S(2)}, u32[]{:S(2)}) collective-permute-start(bf16[4,128,128]{2,1,0:T(8,128)(2,1)S(1)} %pad_maximum_fusion.1.refs_0_), channel_id=1, source_target_pairs={{0,4},{2,6},{4,0},{6,2},{8,12},{10,14},{12,8},{14,10},{16,20},{18,... | collective-permute-start | bytes 393224 | tf_op jit(solution)/shard_map/ppermute | solution.py:238
  15.6 1.4 %collective-permute-start.12 = (bf16[4,128,128]{2,1,0:T(8,128)(2,1)S(1)}, bf16[4,128,128]{2,1,0:T(8,128)(2,1)S(1)}, u32[]{:S(2)}, u32[]{:S(2)}) collective-permute-start(bf16[4,128,128]{2,1,0:T(8,128)(2,1)S(1)} %pad_maximum_fusion.1.refs_0_), channel_id=1, source_target_pairs={{0,6},{2,0},{4,2},{6,4},{8,14},{10,8},{12,10},{14,12},{16,22},{18,... | collective-permute-start | bytes 393224 | tf_op jit(solution)/shard_map/ppermute | solution.py:238
  17.0 1.9 %collective-permute-done.10.refs_1_ = bf16[4,128,128]{2,1,0:T(8,128)(2,1)S(1)} collective-permute-done((bf16[4,128,128]{2,1,0:T(8,128)(2,1)S(1)}, bf16[4,128,128]{2,1,0:T(8,128)(2,1)S(1)}, u32[]{:S(2)}, u32[]{:S(2)}) %collective-permute-start.10) | collective-permute-done | bytes 131104 | tf_op jit(solution)/shard_map/ppermute | solution.py:238
  18.9 1.3 %collective-permute-done.11.refs_2_ = bf16[4,128,128]{2,1,0:T(8,128)(2,1)S(1)} collective-permute-done((bf16[4,128,128]{2,1,0:T(8,128)(2,1)S(1)}, bf16[4,128,128]{2,1,0:T(8,128)(2,1)S(1)}, u32[]{:S(2)}, u32[]{:S(2)}) %collective-permute-start.11) | collective-permute-done | bytes 131104 | tf_op jit(solution)/shard_map/ppermute | solution.py:238
  20.1 0.4 collective-permute-done.12.refs_3_
  20.5 0.0 copy-done
  20.5 0.0 copy-done.2
  20.5 0.0 copy-done.3
  20.5 0.0 copy-start.6
  20.6 1.2 %scale.1.refs_0_ = bf16[128,1024]{1,0:T(8,128)(2,1)S(1)} custom-call(s32[16]{0:T(128)S(1)} %copy-done.2, s32[16]{0:T(128)S(1)} %copy-done.3, bf16[128,1024]{1,0:T(8,128)(2,1)S(1)} %bitcast.11, bf16[4,128,128]{2,1,0:T(8,128)(2,1)S(1)} %pad_maximum_fusion.1.refs_0_, bf16[4,128,128]{2,1,0:T(8,128)(2,1)S(1)} %collective-permute-done.10.refs_1_, ...), custom_call_target="tpu_custom_call" | custom-call | flops 10000000 | bytes 1048576 | tf_op jit(solution)/shard_map/scale/pallas_call | solution.py:288
  21.8 0.0 copy-start.1
  21.8 0.0 copy-start.4
  21.8 0.1 collective-permute-start.13
  21.9 0.0 copy-done.6
  21.9 0.5 %copy-done.1 = f32[64,9]{0,1:T(8,128)S(1)} copy-done((f32[64,9]{0,1:T(8,128)S(1)}, f32[64,9]{0,1:T(8,128)}, u32[]{:S(2)}) %copy-start.1) | copy-done | bytes 2328
  22.5 0.0 copy-start.5
  22.5 0.3 weights.1
  22.8 0.0 collective-permute-done.refs_0_
  22.8 0.0 copy-done.4
  22.8 0.4 copy-done.5
  23.2 2.1 %forward.1 = (bf16[4,128,128]{2,1,0:T(8,128)(2,1)S(1)}, bf16[4,128,128]{2,1,0:T(8,128)(2,1)S(1)}, bf16[4,128,128]{2,1,0:T(8,128)(2,1)S(1)}, bf16[4,128,128]{2,1,0:T(8,128)(2,1)S(1)}) custom-call(s32[8,8]{1,0:T(8,128)S(1)} %copy-done.5, s32[16]{0:T(128)S(1)} %copy-done.2, s32[16]{0:T(128)S(1)} %copy-done.3, bf16[256,1024]{1,0:T(8,128)(2,1)S(1)} %pad_maximum_fusion.both_ref, ...), custom_call_target="tpu_custom_call" | custom-call | flops 1000000000 | bytes 2097152 | tf_op jit(solution)/shard_map/forward/pallas_call | solution.py:261
  25.3 1.4 %collective-permute-start.1 = (bf16[4,128,128]{2,1,0:T(8,128)(2,1)S(1)}, bf16[4,128,128]{2,1,0:T(8,128)(2,1)S(1)}, u32[]{:S(2)}, u32[]{:S(2)}) collective-permute-start(bf16[4,128,128]{2,1,0:T(8,128)(2,1)S(1)} %get-tuple-element.14), channel_id=1, source_target_pairs={{0,2},{2,4},{4,6},{6,0},{8,10},{10,12},{12,14},{14,8},{16,18},{18,... | collective-permute-start | bytes 393224 | tf_op jit(solution)/shard_map/ppermute | solution.py:238
  26.8 1.5 %collective-permute-start.2 = (bf16[4,128,128]{2,1,0:T(8,128)(2,1)S(1)}, bf16[4,128,128]{2,1,0:T(8,128)(2,1)S(1)}, u32[]{:S(2)}, u32[]{:S(2)}) collective-permute-start(bf16[4,128,128]{2,1,0:T(8,128)(2,1)S(1)} %get-tuple-element.15), channel_id=1, source_target_pairs={{0,4},{2,6},{4,0},{6,2},{8,12},{10,14},{12,8},{14,10},{16,20},{18,... | collective-permute-start | bytes 393224 | tf_op jit(solution)/shard_map/ppermute | solution.py:238
  28.3 1.2 %collective-permute-start.3 = (bf16[4,128,128]{2,1,0:T(8,128)(2,1)S(1)}, bf16[4,128,128]{2,1,0:T(8,128)(2,1)S(1)}, u32[]{:S(2)}, u32[]{:S(2)}) collective-permute-start(bf16[4,128,128]{2,1,0:T(8,128)(2,1)S(1)} %get-tuple-element.16), channel_id=1, source_target_pairs={{0,6},{2,0},{4,2},{6,4},{8,14},{10,8},{12,10},{14,12},{16,22},{18,... | collective-permute-start | bytes 393224 | tf_op jit(solution)/shard_map/ppermute | solution.py:238
  29.4 3.2 %collective-permute-done.1.refs_1_ = bf16[4,128,128]{2,1,0:T(8,128)(2,1)S(1)} collective-permute-done((bf16[4,128,128]{2,1,0:T(8,128)(2,1)S(1)}, bf16[4,128,128]{2,1,0:T(8,128)(2,1)S(1)}, u32[]{:S(2)}, u32[]{:S(2)}) %collective-permute-start.1) | collective-permute-done | bytes 131104 | tf_op jit(solution)/shard_map/ppermute | solution.py:238
  32.7 1.8 %collective-permute-done.2.refs_2_ = bf16[4,128,128]{2,1,0:T(8,128)(2,1)S(1)} collective-permute-done((bf16[4,128,128]{2,1,0:T(8,128)(2,1)S(1)}, bf16[4,128,128]{2,1,0:T(8,128)(2,1)S(1)}, u32[]{:S(2)}, u32[]{:S(2)}) %collective-permute-start.2) | collective-permute-done | bytes 131104 | tf_op jit(solution)/shard_map/ppermute | solution.py:238
  34.4 0.0 collective-permute-done.3.refs_3_
  34.4 0.1 partial.1
  34.5 0.1 collective-permute-start.4
  34.6 1.2 %collective-permute-start.5 = (bf16[128,128]{1,0:T(8,128)(2,1)S(1)}, bf16[128,128]{1,0:T(8,128)(2,1)S(1)}, u32[]{:S(2)}, u32[]{:S(2)}) collective-permute-start(bf16[128,128]{1,0:T(8,128)(2,1)S(1)} %get-tuple-element.19), channel_id=1, source_target_pairs={{0,16},{2,18},{4,20},{6,22},{8,24},{10,26},{12,28},{14,30},{16,0},... | collective-permute-start | bytes 98312 | tf_op jit(solution)/shard_map/ppermute | solution.py:230
  35.8 2.8 %collective-permute-start.6 = (bf16[128,128]{1,0:T(8,128)(2,1)S(1)}, bf16[128,128]{1,0:T(8,128)(2,1)S(1)}, u32[]{:S(2)}, u32[]{:S(2)}) collective-permute-start(bf16[128,128]{1,0:T(8,128)(2,1)S(1)} %get-tuple-element.20), channel_id=1, source_target_pairs={{0,24},{2,26},{4,28},{6,30},{8,0},{10,2},{12,4},{14,6},{16,8},{18,... | collective-permute-start | bytes 98312 | tf_op jit(solution)/shard_map/ppermute | solution.py:230
  38.6 0.0 collective-permute-done.13.refs_1_
  38.6 2.4 %backward.1 = bf16[128,1024]{1,0:T(8,128)(2,1)} custom-call(s32[8,8]{1,0:T(8,128)S(1)} %copy-done.5, bf16[2,128,256]{2,1,0:T(8,128)(2,1)S(1)} %get-tuple-element.21.up_ref, bf16[1024,128]{1,0:T(8,128)(2,1)S(1)} %bitcast.15, bf16[128,1024]{1,0:T(8,128)(2,1)S(1)} %scale.1.refs_0_, bf16[128,1024]{1,0:T(8,128)(2,1)S(1)} %collective-permute-done.13.refs_1_), custom_call_target="tpu_custom_call" | custom-call | flops 1000000000 | bytes 1048576 | tf_op jit(solution)/shard_map/backward/pallas_call | solution.py:302
  41.0 0.0 collective-permute-done.4.refs_1_
  41.0 0.0 collective-permute-done.5.refs_2_
  41.0 0.0 collective-permute-done.6.refs_3_
  41.0 0.6 %total.1 = bf16[128,128]{1,0:T(8,128)(2,1)} custom-call(bf16[128,128]{1,0:T(8,128)(2,1)S(1)} %get-tuple-element.17.refs_0_, bf16[128,128]{1,0:T(8,128)(2,1)S(1)} %collective-permute-done.4.refs_1_, bf16[128,128]{1,0:T(8,128)(2,1)S(1)} %collective-permute-done.5.refs_2_, bf16[128,128]{1,0:T(8,128)(2,1)S(1)} %collective-permute-done.6.refs_3_), custom_call_target="tpu_custom_call" | custom-call | flops 1000000 | bytes 262144 | tf_op jit(solution)/shard_map/total/pallas_call | solution.py:316
  (1 shorter events, 0.0 us)
Async XLA Ops:
  0.6 19.9 %copy-start = (bf16[1,4,32,1024]{3,2,1,0:T(8,128)(2,1)S(1)}, bf16[1,4,32,1024]{3,2,1,0:T(8,128)(2,1)}, u32[]{:S(2)}) copy-start(bf16[1,4,32,1024]{3,2,1,0:T(8,128)(2,1)} %param.9) | copy-start | bytes 786436
  0.6 7.0 %collective-permute-start.9 = (bf16[128,128]{1,0:T(8,128)(2,1)}, bf16[128,128]{1,0:T(8,128)(2,1)S(1)}, u32[]{:S(2)}, u32[]{:S(2)}) collective-permute-start(bf16[128,128]{1,0:T(8,128)(2,1)} %bitcast.19), channel_id=1, source_target_pairs={{0,24},{2,26},{4,28},{6,30},{8,0},{10,2},{12,4},{14,6},{16,8},{18,... | collective-permute-start | bytes 98312 | tf_op jit(solution)/shard_map/ppermute | solution.py:230
  5.8 5.0 %collective-permute-start.8 = (bf16[128,128]{1,0:T(8,128)(2,1)}, bf16[128,128]{1,0:T(8,128)(2,1)S(1)}, u32[]{:S(2)}, u32[]{:S(2)}) collective-permute-start(bf16[128,128]{1,0:T(8,128)(2,1)} %bitcast.20), channel_id=1, source_target_pairs={{0,16},{2,18},{4,20},{6,22},{8,24},{10,26},{12,28},{14,30},{16,0},... | collective-permute-start | bytes 98312 | tf_op jit(solution)/shard_map/ppermute | solution.py:230
  5.8 5.9 %collective-permute-start.7 = (bf16[128,128]{1,0:T(8,128)(2,1)}, bf16[128,128]{1,0:T(8,128)(2,1)S(1)}, u32[]{:S(2)}, u32[]{:S(2)}) collective-permute-start(bf16[128,128]{1,0:T(8,128)(2,1)} %bitcast.21), channel_id=1, source_target_pairs={{0,8},{2,10},{4,12},{6,14},{8,16},{10,18},{12,20},{14,22},{16,24},... | collective-permute-start | bytes 98312 | tf_op jit(solution)/shard_map/ppermute | solution.py:230
  6.8 16.0 %collective-permute-start = (bf16[128,1024]{1,0:T(8,128)(2,1)}, bf16[128,1024]{1,0:T(8,128)(2,1)S(1)}, u32[]{:S(2)}, u32[]{:S(2)}) collective-permute-start(bf16[128,1024]{1,0:T(8,128)(2,1)} %bitcast.16), channel_id=1, source_target_pairs={{0,1},{1,0},{2,3},{3,2},{4,5},{5,4},{6,7},{7,6},{8,9},{9,8},{10,11... | collective-permute-start | bytes 786440 | tf_op jit(solution)/shard_map/ppermute | solution.py:21
  12.5 8.1 %copy-start.2 = (s32[16]{0:T(128)S(1)}, s32[16]{0:T(128)}, u32[]{:S(2)}) copy-start(s32[16]{0:T(128)} %sizes_ref.3) | copy-start | bytes 196
  12.5 8.1 %copy-start.3 = (s32[16]{0:T(128)S(1)}, s32[16]{0:T(128)}, u32[]{:S(2)}) copy-start(s32[16]{0:T(128)} %owner_ref.3) | copy-start | bytes 196
  12.5 6.4 %collective-permute-start.10 = (bf16[4,128,128]{2,1,0:T(8,128)(2,1)S(1)}, bf16[4,128,128]{2,1,0:T(8,128)(2,1)S(1)}, u32[]{:S(2)}, u32[]{:S(2)}) collective-permute-start(bf16[4,128,128]{2,1,0:T(8,128)(2,1)S(1)} %pad_maximum_fusion.1.refs_0_), channel_id=1, source_target_pairs={{0,2},{2,4},{4,6},{6,0},{8,10},{10,12},{12,14},{14,8},{16,18},{18,... | collective-permute-start | bytes 393224 | tf_op jit(solution)/shard_map/ppermute | solution.py:238
  14.0 6.1 %collective-permute-start.11 = (bf16[4,128,128]{2,1,0:T(8,128)(2,1)S(1)}, bf16[4,128,128]{2,1,0:T(8,128)(2,1)S(1)}, u32[]{:S(2)}, u32[]{:S(2)}) collective-permute-start(bf16[4,128,128]{2,1,0:T(8,128)(2,1)S(1)} %pad_maximum_fusion.1.refs_0_), channel_id=1, source_target_pairs={{0,4},{2,6},{4,0},{6,2},{8,12},{10,14},{12,8},{14,10},{16,20},{18,... | collective-permute-start | bytes 393224 | tf_op jit(solution)/shard_map/ppermute | solution.py:238
  15.6 5.0 %collective-permute-start.12 = (bf16[4,128,128]{2,1,0:T(8,128)(2,1)S(1)}, bf16[4,128,128]{2,1,0:T(8,128)(2,1)S(1)}, u32[]{:S(2)}, u32[]{:S(2)}) collective-permute-start(bf16[4,128,128]{2,1,0:T(8,128)(2,1)S(1)} %pad_maximum_fusion.1.refs_0_), channel_id=1, source_target_pairs={{0,6},{2,0},{4,2},{6,4},{8,14},{10,8},{12,10},{14,12},{16,22},{18,... | collective-permute-start | bytes 393224 | tf_op jit(solution)/shard_map/ppermute | solution.py:238
  20.5 1.4 %copy-start.6 = (bf16[1,4,32,1024]{3,2,1,0:T(8,128)(2,1)S(1)}, bf16[1,4,32,1024]{3,2,1,0:T(8,128)(2,1)}, u32[]{:S(2)}) copy-start(bf16[1,4,32,1024]{3,2,1,0:T(8,128)(2,1)} %param.8) | copy-start | bytes 786436
  21.8 0.7 %copy-start.1 = (f32[64,9]{0,1:T(8,128)S(1)}, f32[64,9]{0,1:T(8,128)}, u32[]{:S(2)}) copy-start(f32[64,9]{0,1:T(8,128)} %param.11) | copy-start | bytes 6916
  21.8 1.0 %copy-start.4 = (bf16[8,128,128]{2,1,0:T(8,128)(2,1)S(1)}, bf16[8,128,128]{2,1,0:T(8,128)(2,1)}, u32[]{:S(2)}) copy-start(bf16[8,128,128]{2,1,0:T(8,128)(2,1)} %param.10) | copy-start | bytes 786436
  21.8 16.8 %collective-permute-start.13 = (bf16[128,1024]{1,0:T(8,128)(2,1)S(1)}, bf16[128,1024]{1,0:T(8,128)(2,1)S(1)}, u32[]{:S(2)}, u32[]{:S(2)}) collective-permute-start(bf16[128,1024]{1,0:T(8,128)(2,1)S(1)} %scale.1.refs_0_), channel_id=1, source_target_pairs={{0,1},{1,0},{2,3},{3,2},{4,5},{5,4},{6,7},{7,6},{8,9},{9,8},{10,11... | collective-permute-start | bytes 786440 | tf_op jit(solution)/shard_map/ppermute | solution.py:21
  22.5 0.7 %copy-start.5 = (s32[8,8]{1,0:T(8,128)S(1)}, s32[8,8]{1,0:T(8,128)}, u32[]{:S(2)}) copy-start(s32[8,8]{1,0:T(8,128)} %pattern_ref.3) | copy-start | bytes 772
  25.3 7.3 %collective-permute-start.1 = (bf16[4,128,128]{2,1,0:T(8,128)(2,1)S(1)}, bf16[4,128,128]{2,1,0:T(8,128)(2,1)S(1)}, u32[]{:S(2)}, u32[]{:S(2)}) collective-permute-start(bf16[4,128,128]{2,1,0:T(8,128)(2,1)S(1)} %get-tuple-element.14), channel_id=1, source_target_pairs={{0,2},{2,4},{4,6},{6,0},{8,10},{10,12},{12,14},{14,8},{16,18},{18,... | collective-permute-start | bytes 393224 | tf_op jit(solution)/shard_map/ppermute | solution.py:238
  26.8 7.7 %collective-permute-start.2 = (bf16[4,128,128]{2,1,0:T(8,128)(2,1)S(1)}, bf16[4,128,128]{2,1,0:T(8,128)(2,1)S(1)}, u32[]{:S(2)}, u32[]{:S(2)}) collective-permute-start(bf16[4,128,128]{2,1,0:T(8,128)(2,1)S(1)} %get-tuple-element.15), channel_id=1, source_target_pairs={{0,4},{2,6},{4,0},{6,2},{8,12},{10,14},{12,8},{14,10},{16,20},{18,... | collective-permute-start | bytes 393224 | tf_op jit(solution)/shard_map/ppermute | solution.py:238
  28.3 6.2 %collective-permute-start.3 = (bf16[4,128,128]{2,1,0:T(8,128)(2,1)S(1)}, bf16[4,128,128]{2,1,0:T(8,128)(2,1)S(1)}, u32[]{:S(2)}, u32[]{:S(2)}) collective-permute-start(bf16[4,128,128]{2,1,0:T(8,128)(2,1)S(1)} %get-tuple-element.16), channel_id=1, source_target_pairs={{0,6},{2,0},{4,2},{6,4},{8,14},{10,8},{12,10},{14,12},{16,22},{18,... | collective-permute-start | bytes 393224 | tf_op jit(solution)/shard_map/ppermute | solution.py:238
  34.5 6.5 %collective-permute-start.4 = (bf16[128,128]{1,0:T(8,128)(2,1)S(1)}, bf16[128,128]{1,0:T(8,128)(2,1)S(1)}, u32[]{:S(2)}, u32[]{:S(2)}) collective-permute-start(bf16[128,128]{1,0:T(8,128)(2,1)S(1)} %get-tuple-element.18), channel_id=1, source_target_pairs={{0,8},{2,10},{4,12},{6,14},{8,16},{10,18},{12,20},{14,22},{16,24},... | collective-permute-start | bytes 98312 | tf_op jit(solution)/shard_map/ppermute | solution.py:230
  34.6 6.4 %collective-permute-start.5 = (bf16[128,128]{1,0:T(8,128)(2,1)S(1)}, bf16[128,128]{1,0:T(8,128)(2,1)S(1)}, u32[]{:S(2)}, u32[]{:S(2)}) collective-permute-start(bf16[128,128]{1,0:T(8,128)(2,1)S(1)} %get-tuple-element.19), channel_id=1, source_target_pairs={{0,16},{2,18},{4,20},{6,22},{8,24},{10,26},{12,28},{14,30},{16,0},... | collective-permute-start | bytes 98312 | tf_op jit(solution)/shard_map/ppermute | solution.py:230
  35.8 5.2 %collective-permute-start.6 = (bf16[128,128]{1,0:T(8,128)(2,1)S(1)}, bf16[128,128]{1,0:T(8,128)(2,1)S(1)}, u32[]{:S(2)}, u32[]{:S(2)}) collective-permute-start(bf16[128,128]{1,0:T(8,128)(2,1)S(1)} %get-tuple-element.20), channel_id=1, source_target_pairs={{0,24},{2,26},{4,28},{6,30},{8,0},{10,2},{12,4},{14,6},{16,8},{18,... | collective-permute-start | bytes 98312 | tf_op jit(solution)/shard_map/ppermute | solution.py:230

commit v4 on v3

--- a/solution.py
+++ b/solution.py
@@ -12,7 +12,7 @@
 VREACH = 4
 LANES = 128
 VMEM = pl.BlockSpec(memory_space=pltpu.VMEM)
-SMEM = pl.BlockSpec(memory_space=pltpu.SMEM)
+ANY = pl.BlockSpec(memory_space=pl.ANY)
 
 
 def neighbour_slabs(block):
@@ -31,12 +31,28 @@
     return [0, -1, 1]
 
 
+def can_pair(count):
+    return count & (count - 1) == 0
+
+
+def plane_target(index, step, count):
+    return index ^ step if can_pair(count) else (index + step) % count
+
+
+def plane_step(source, target, count):
+    return source ^ target if can_pair(count) else (target - source + count) % count
+
+
+def line_step(source, target, count):
+    return (target - source + count) % count
+
+
 def split_bf16(value):
     high = value.astype(jnp.bfloat16)
     return high, (value - high.astype(jnp.float32)).astype(jnp.bfloat16)
 
 
-def weight_kernel(fields, slabs, vloc_ref, down_ref, up_ref, taps):
+def vertical_weights(fields, slabs, vloc_ref, down_ref, up_ref, taps):
     slab = lax.axis_index("lev")
     reach = VREACH
     levels = vloc_ref.shape[1] // slabs
@@ -76,6 +92,16 @@
         )
 
 
+def start_loads(sources, targets, sems):
+    loads = [
+        pltpu.make_async_copy(source, target, sems.at[i])
+        for i, (source, target) in enumerate(zip(sources, targets))
+    ]
+    for load in loads:
+        load.start()
+    return loads
+
+
 def region_loop(sizes_ref, owner_ref, width, body):
     def step(region, start):
         size = sizes_ref[region]
@@ -85,16 +111,20 @@
     lax.fori_loop(0, sizes_ref.shape[0], step, jnp.int32(0), unroll=4)
 
 
-def forward_kernel(grid, pattern_ref, sizes_ref, owner_ref, both_ref, down_ref, htile_ref, *refs):
+def forward_kernel(
+    grid, fields, slabs, pattern, sizes, owner, both_ref, vloc_ref, htile_ref, *refs
+):
     outer, inner = grid
-    out_refs = refs[-inner - 3 : -3]
-    slab_refs = refs[: -inner - 3]
-    mixed, product, placed = refs[-3:]
+    pattern_ref, sizes_ref, owner_ref, sems, down_ref, taps, mixed, product, placed = refs[-9:]
+    loads = start_loads((pattern, sizes, owner), (pattern_ref, sizes_ref, owner_ref), sems)
+    up_ref = refs[-10]
+    out_refs = refs[-inner - 10 : -10]
+    vertical_weights(fields, slabs, vloc_ref, down_ref, up_ref, taps)
     blocks, slots = pattern_ref.shape
-    rows = both_ref.shape[0] // 2
-    ens_ref = both_ref.at[rows:]
+    span, rows = down_ref.shape[1:]
+    ens_ref = both_ref.at[span:]
     width = htile_ref.shape[1]
-    extended = jnp.concatenate([both_ref[:rows]] + [ref[...] for ref in slab_refs], axis=0)
+    extended = both_ref[:span]
     dims = (((0,), (0,)), ((), ()))
     summed = lax.dot_general(down_ref[0], extended, dims, preferred_element_type=jnp.float32)
     summed = summed + lax.dot_general(
@@ -103,6 +133,9 @@
     for b in range(blocks):
         mixed[b] = summed[:, b * width : (b + 1) * width].astype(jnp.bfloat16)
 
+    for load in loads:
+        load.wait()
+
     def spread(b, carry):
         picked = jnp.concatenate([mixed[pattern_ref[b, k]] for k in range(slots)], axis=1)
         localized = jnp.dot(picked, htile_ref[...], preferred_element_type=jnp.float32)
@@ -120,7 +153,8 @@
         both = jnp.where(lane >= shift, product[block], product[block + 1])
         turned = pltpu.roll(both, (width - shift) % width, 1)
         kept = jnp.where(lane < size, turned, 0.0).astype(jnp.bfloat16)
-        placed[(owner % inner - here + inner) % inner, (owner // inner - line + outer) % outer] = kept
+        step = plane_step(here, owner % inner, inner), line_step(line, owner // inner, outer)
+        placed[step] = kept
 
     region_loop(sizes_ref, owner_ref, width, place)
     for i in range(inner):
@@ -140,13 +174,18 @@
         gathered[i] = cot_refs[i][...]
     columns_of[0] = jnp.zeros((rows, width), jnp.float32)
 
-    def place(owner, block, shift, size):
-        region = gathered[(here - owner % inner + inner) % inner, (line - owner // inner + outer) % outer]
+    def place(owner, block, shift):
+        step = plane_step(owner % inner, here, inner), line_step(owner // inner, line, outer)
+        region = gathered[step]
         turned = pltpu.roll(region.astype(jnp.float32), shift, 1)
         columns_of[block] = jnp.where(lane >= shift, turned, columns_of[block])
         columns_of[block + 1] = turned
 
-    region_loop(sizes_ref, owner_ref, width, place)
+    sizes, owners = sizes_ref[...], owner_ref[...]
+    start = jnp.int32(0)
+    for region in range(sizes.shape[1]):
+        place(owners[0, region], start // width, start % width)
+        start = start + sizes[0, region]
     for b in range(blocks):
         part = slice(b * width, (b + 1) * width)
         out_ref[:, part] = (ens_ref[:, part].astype(jnp.float32) * columns_of[b]).astype(
@@ -154,9 +193,14 @@
         )
 
 
-def backward_kernel(pattern_ref, up_ref, htile_ref, *refs):
-    slab_refs = refs[:-3]
-    out_ref, mixed, total = refs[-3:]
+def backward_kernel(outer, scale, pattern, up_ref, htile_ref, *refs):
+    slab_refs, term_refs = refs[: -outer - 6], refs[-outer - 6 : -6]
+    increment_ref, out_ref, pattern_ref, sems, mixed, total = refs[-6:]
+    (load,) = start_loads((pattern,), (pattern_ref,), sems)
+    summed = term_refs[0][...].astype(jnp.float32)
+    for term in term_refs[1:]:
+        summed = summed + term[...].astype(jnp.float32)
+    increment_ref[...] = (summed * scale).astype(jnp.bfloat16)
     blocks, slots = pattern_ref.shape
     rows = out_ref.shape[0]
     width = htile_ref.shape[1]
@@ -167,13 +211,18 @@
         mixed[b] = summed[:, b * width : (b + 1) * width].astype(jnp.bfloat16)
         total[b] = jnp.zeros((rows, width), jnp.float32)
 
+    load.wait()
+
     def gather(b, carry):
-        spread = lax.dot_general(
-            mixed[b], htile_ref[...], (((1,), (1,)), ((), ())), preferred_element_type=jnp.float32
-        )
-        for k in range(slots):
-            target = pattern_ref[b, k]
-            total[target] = total[target] + spread[:, k * width : (k + 1) * width]
+        for first in range(0, slots, 2):
+            tiles = htile_ref[first * width : (first + 2) * width]
+            spread = lax.dot_general(
+                mixed[b], tiles, (((1,), (1,)), ((), ())), preferred_element_type=jnp.float32
+            )
+            for k in range(first, min(first + 2, slots)):
+                target = pattern_ref[b, k]
+                part = spread[:, (k - first) * width : (k - first + 1) * width]
+                total[target] = total[target] + part
         return carry
 
     lax.fori_loop(0, blocks, gather, 0, unroll=min(blocks, 8))
@@ -189,13 +238,6 @@
         for part in parts[1:]:
             total = total + part[i].astype(jnp.float32)
         outs[i][...] = total.astype(outs[i].dtype)
-
-
-def total_kernel(scale, *refs):
-    total = refs[0][...].astype(jnp.float32)
-    for part in refs[1:-1]:
-        total = total + part[...].astype(jnp.float32)
-    refs[-1][...] = (total * scale).astype(jnp.bfloat16)
 
 
 PARAMS = pltpu.CompilerParams(vmem_limit_bytes=8 << 20)
@@ -231,7 +273,7 @@
 
     def in_plane(value, step):
         pairs = [
-            (o * inner + i, o * inner + (i + step) % inner)
+            (o * inner + i, o * inner + plane_target(i, step, inner))
             for o in range(outer)
             for i in range(inner)
         ]
@@ -246,24 +288,19 @@
     cot_line = jnp.stack([cot_rows] + [along_line(cot_rows, i) for i in range(1, outer)])
     cot_parts = [cot_line] + [in_plane(cot_line, i) for i in range(1, inner)]
 
-    both = lax.concatenate([alpha_rows, ens_rows], 0)
-    down, up = pl.pallas_call(
-        functools.partial(weight_kernel, fields, slabs),
-        out_shape=(bf16((2, span, rows)), bf16((2, rows, span))),
-        in_specs=[VMEM],
-        out_specs=(VMEM, VMEM),
-        scratch_shapes=[pltpu.VMEM((2 * 8, LANES), jnp.float32)],
-        compiler_params=PARAMS,
-        cost_estimate=cost(10**6, 10**5),
-        name="weights",
-    )(vloc.T)
-
+    both = lax.concatenate([*alpha_slabs, ens_rows], 0)
     sent = pl.pallas_call(
-        functools.partial(forward_kernel, grid),
-        out_shape=[bf16((outer, rows, width))] * inner,
-        in_specs=[SMEM] * 3 + [VMEM] * (2 + len(alpha_slabs)),
-        out_specs=[VMEM] * inner,
+        functools.partial(forward_kernel, grid, fields, slabs),
+        out_shape=[bf16((outer, rows, width))] * inner + [bf16((2, rows, span))],
+        in_specs=[ANY] * 3 + [VMEM] * 3,
+        out_specs=[VMEM] * (inner + 1),
         scratch_shapes=[
+            pltpu.SMEM(pattern.shape, jnp.int32),
+            pltpu.SMEM(region_sizes.shape, jnp.int32),
+            pltpu.SMEM(owner.shape, jnp.int32),
+            pltpu.SemaphoreType.DMA((3,)),
+            pltpu.VMEM((2, span, rows), jnp.bfloat16),
+            pltpu.VMEM((2 * 8, LANES), jnp.float32),
             pltpu.VMEM((blocks, rows, width), jnp.bfloat16),
             pltpu.VMEM((blocks + 1, rows, width), jnp.float32),
             pltpu.VMEM((inner, outer, rows, width), jnp.bfloat16),
@@ -271,7 +308,8 @@
         compiler_params=PARAMS,
         cost_estimate=cost(10**9, 2 << 20),
         name="forward",
-    )(pattern, region_sizes, owner, both, down, stacked, *alpha_slabs[1:])
+    )(pattern, region_sizes, owner, both, vloc.T, stacked)
+    *sent, up = sent
 
     arrived = [sent[0]] + [in_plane(sent[i], i) for i in range(1, inner)]
     partial = pl.pallas_call(
@@ -288,7 +326,7 @@
     scaled = pl.pallas_call(
         functools.partial(scale_kernel, grid),
         out_shape=bf16((rows, columns)),
-        in_specs=[SMEM] * 2 + [VMEM] * (1 + inner),
+        in_specs=[VMEM] * 2 + [VMEM] * (1 + inner),
         out_specs=VMEM,
         scratch_shapes=[
             pltpu.VMEM((inner, outer, rows, width), jnp.bfloat16),
@@ -297,31 +335,24 @@
         compiler_params=PARAMS,
         cost_estimate=cost(10**7, 1 << 20),
         name="scale",
-    )(region_sizes, owner, ens_rows, *cot_parts)
+    )(region_sizes[None], owner[None], ens_rows, *cot_parts)
     scaled_slabs = [scaled] + neighbour_slabs(scaled)
-    gradient = pl.pallas_call(
-        backward_kernel,
-        out_shape=bf16((rows, columns)),
-        in_specs=[SMEM] + [VMEM] * (2 + len(scaled_slabs)),
-        out_specs=VMEM,
+    increment, gradient = pl.pallas_call(
+        functools.partial(backward_kernel, outer, member_scale),
+        out_shape=[bf16((rows, width)), bf16((rows, columns))],
+        in_specs=[ANY] + [VMEM] * (2 + len(scaled_slabs) + outer),
+        out_specs=[VMEM] * 2,
         scratch_shapes=[
+            pltpu.SMEM(pattern.shape, jnp.int32),
+            pltpu.SemaphoreType.DMA((1,)),
             pltpu.VMEM((blocks, rows, width), jnp.bfloat16),
             pltpu.VMEM((blocks, rows, width), jnp.float32),
         ],
         compiler_params=PARAMS,
         cost_estimate=cost(10**9, 1 << 20),
         name="backward",
-    )(pattern, up, stacked, *scaled_slabs)
-
-    increment = pl.pallas_call(
-        functools.partial(total_kernel, member_scale),
-        out_shape=bf16((rows, width)),
-        in_specs=[VMEM] * outer,
-        out_specs=VMEM,
-        compiler_params=PARAMS,
-        cost_estimate=cost(10**6, 1 << 18),
-        name="total",
-    )(*terms)
+    )(pattern, up, stacked, *scaled_slabs, *terms)
+
     return (
         increment.reshape(fields, levels, width),
         gradient.reshape(members, fields, levels, columns),

time: 41.9 us -> 44.6 us (1.064)
  waiting for transfers between devices: 13.5 us -> 17.3 us
  local copies, waits for them, and re-layouts: 0.94 us -> 3.08 us
  Pallas kernels: 6.75 us -> 4.86 us
  starting transfers between devices: 18.9 us -> 17.5 us
    unnamed x14 -> x20, local copies, waits for them, and re-layouts: 0.94 us -> 3.08 us
    ppermute x6, waiting for transfers between devices: 4.92 us -> 7.05 us  [along_line(): return lax.ppermute(value, 'wide', pairs)]
    ppermute x6, waiting for transfers between devices: 8.53 us -> 10.3 us  [in_plane(): return lax.ppermute(value, 'wide', pairs)]
    ppermute x6, starting transfers between devices: 8.6 us -> 7.11 us  [in_plane(): return lax.ppermute(value, 'wide', pairs)]
    pallas_call x4 -> x2, Pallas kernels: 5.45 us -> 4.26 us  [the longest x1 2.19 us: body(): pl.pallas_call(functools.partial(backward_kernel, outer, member_scale), o...]
    pallas_call x1, Pallas kernels: 1.23 us -> 0.53 us  [body(): pl.pallas_call(functools.partial(scale_kernel, grid), out_shape=bf16((row...]
  transfers between devices with their start and end apart: 14 -> 14, of which waited for: 8 -> 11; matrix products, arithmetic and copies ran while one was open for 2% -> 2% of each run, Pallas kernels for 15% -> 6%
where the time goes in v4:
time: 44.6 us; the launch traced here: 44.3 us
  starting transfers between devices  17.5 us (39%)
  waiting for transfers between devices  17.3 us (39%)
  Pallas kernels  4.86 us (11%)
  local copies, waits for them, and re-layouts  3.08 us (7%)
  other arithmetic  0.83 us (2%)
  between operations  0.75 us (2%)
    ppermute x6, starting transfers between devices, along_line(): return lax.ppermute(value, 'wide', pairs)  10.3 us
    ppermute x6, waiting for transfers between devices, in_plane(): return lax.ppermute(value, 'wide', pairs)  10.3 us
    ppermute x6, starting transfers between devices, in_plane(): return lax.ppermute(value, 'wide', pairs)  7.11 us
    ppermute x6, waiting for transfers between devices, along_line(): return lax.ppermute(value, 'wide', pairs)  7.05 us
    unnamed x20, local copies, waits for them, and re-layouts  3.08 us
    pallas_call x1, Pallas kernels, body(): pl.pallas_call(functools.partial(backward_kernel, outer, member_scale), o...  2.19 us
    pallas_call x1, Pallas kernels, body(): pl.pallas_call(functools.partial(forward_kernel, grid, fields, slabs), ou...  2.07 us
  transfers between devices with their start and end apart: 14, of which 11 were waited for; matrix products, arithmetic and copies ran while one was open for 2% of the time, Pallas kernels for 6%

profile of v4, /device:TPU:0, one launch (start us, length us, event | category | flops | bytes accessed | tf_op | source)
XLA Modules:
  0.0 44.3 jit_solution(14423175932427198525)
XLA Ops:
  0.6 0.0 copy-start.1
  0.6 5.1 %collective-permute-start.3 = (bf16[128,128]{1,0:T(8,128)(2,1)}, bf16[128,128]{1,0:T(8,128)(2,1)S(1)}, u32[]{:S(2)}, u32[]{:S(2)}) collective-permute-start(bf16[128,128]{1,0:T(8,128)(2,1)} %bitcast.22), channel_id=1, source_target_pairs={{0,24},{2,26},{4,28},{6,30},{8,0},{10,2},{12,4},{14,6},{16,8},{18,... | collective-permute-start | bytes 98312 | tf_op jit(solution)/shard_map/ppermute | solution.py:272
  5.8 0.0 collective-permute-start.2
  5.8 1.0 %collective-permute-start.1 = (bf16[128,128]{1,0:T(8,128)(2,1)}, bf16[128,128]{1,0:T(8,128)(2,1)S(1)}, u32[]{:S(2)}, u32[]{:S(2)}) collective-permute-start(bf16[128,128]{1,0:T(8,128)(2,1)} %bitcast.24), channel_id=1, source_target_pairs={{0,8},{2,10},{4,12},{6,14},{8,16},{10,18},{12,20},{14,22},{16,24},... | collective-permute-start | bytes 98312 | tf_op jit(solution)/shard_map/ppermute | solution.py:272
  6.8 0.0 collective-permute-start
  6.8 0.9 %collective-permute-done.3 = bf16[128,128]{1,0:T(8,128)(2,1)S(1)} collective-permute-done((bf16[128,128]{1,0:T(8,128)(2,1)}, bf16[128,128]{1,0:T(8,128)(2,1)S(1)}, u32[]{:S(2)}, u32[]{:S(2)}) %collective-permute-start.3) | collective-permute-done | bytes 32800 | tf_op jit(solution)/shard_map/ppermute | solution.py:272
  7.7 3.1 %collective-permute-done.2 = bf16[128,128]{1,0:T(8,128)(2,1)S(1)} collective-permute-done((bf16[128,128]{1,0:T(8,128)(2,1)}, bf16[128,128]{1,0:T(8,128)(2,1)S(1)}, u32[]{:S(2)}, u32[]{:S(2)}) %collective-permute-start.2) | collective-permute-done | bytes 32800 | tf_op jit(solution)/shard_map/ppermute | solution.py:272
  10.8 0.9 %collective-permute-done.1 = bf16[128,128]{1,0:T(8,128)(2,1)S(1)} collective-permute-done((bf16[128,128]{1,0:T(8,128)(2,1)}, bf16[128,128]{1,0:T(8,128)(2,1)S(1)}, u32[]{:S(2)}, u32[]{:S(2)}) %collective-permute-start.1) | collective-permute-done | bytes 32800 | tf_op jit(solution)/shard_map/ppermute | solution.py:272
  11.7 0.8 %pad_maximum_fusion.1.refs_0_ = bf16[4,128,128]{2,1,0:T(8,128)(2,1)S(1)} fusion(bf16[1,128,128]{2,1,0:T(8,128)(2,1)S(1)} %bitcast.26, bf16[1,128,128]{2,1,0:T(8,128)(2,1)S(1)} %bitcast.27, bf16[1,128,128]{2,1,0:T(8,128)(2,1)S(1)} %bitcast.28, bf16[1,128,128]{2,1,0:T(8,128)(2,1)} %bitcast.25), kind=kLoop, calls=%fused_computation.1 | loop fusion | flops 196608 | bytes 262144 | tf_op jit(solution)/shard_map/stack | solution.py:288
  12.5 1.6 %collective-permute-start.4 = (bf16[4,128,128]{2,1,0:T(8,128)(2,1)S(1)}, bf16[4,128,128]{2,1,0:T(8,128)(2,1)S(1)}, u32[]{:S(2)}, u32[]{:S(2)}) collective-permute-start(bf16[4,128,128]{2,1,0:T(8,128)(2,1)S(1)} %pad_maximum_fusion.1.refs_0_), channel_id=1, source_target_pairs={{0,2},{2,0},{4,6},{6,4},{8,10},{10,8},{12,14},{14,12},{16,18},{18,... | collective-permute-start | bytes 393224 | tf_op jit(solution)/shard_map/ppermute | solution.py:280
  14.0 1.5 %collective-permute-start.5 = (bf16[4,128,128]{2,1,0:T(8,128)(2,1)S(1)}, bf16[4,128,128]{2,1,0:T(8,128)(2,1)S(1)}, u32[]{:S(2)}, u32[]{:S(2)}) collective-permute-start(bf16[4,128,128]{2,1,0:T(8,128)(2,1)S(1)} %pad_maximum_fusion.1.refs_0_), channel_id=1, source_target_pairs={{0,4},{2,6},{4,0},{6,2},{8,12},{10,14},{12,8},{14,10},{16,20},{18,... | collective-permute-start | bytes 393224 | tf_op jit(solution)/shard_map/ppermute | solution.py:280
  15.6 0.5 %collective-permute-start.6 = (bf16[4,128,128]{2,1,0:T(8,128)(2,1)S(1)}, bf16[4,128,128]{2,1,0:T(8,128)(2,1)S(1)}, u32[]{:S(2)}, u32[]{:S(2)}) collective-permute-start(bf16[4,128,128]{2,1,0:T(8,128)(2,1)S(1)} %pad_maximum_fusion.1.refs_0_), channel_id=1, source_target_pairs={{0,6},{2,4},{4,2},{6,0},{8,14},{10,12},{12,10},{14,8},{16,22},{18,... | collective-permute-start | bytes 393224 | tf_op jit(solution)/shard_map/ppermute | solution.py:280
  16.0 2.7 %collective-permute-done.4.refs_1_ = bf16[4,128,128]{2,1,0:T(8,128)(2,1)S(1)} collective-permute-done((bf16[4,128,128]{2,1,0:T(8,128)(2,1)S(1)}, bf16[4,128,128]{2,1,0:T(8,128)(2,1)S(1)}, u32[]{:S(2)}, u32[]{:S(2)}) %collective-permute-start.4) | collective-permute-done | bytes 131104 | tf_op jit(solution)/shard_map/ppermute | solution.py:280
  18.7 1.2 %collective-permute-done.5.refs_2_ = bf16[4,128,128]{2,1,0:T(8,128)(2,1)S(1)} collective-permute-done((bf16[4,128,128]{2,1,0:T(8,128)(2,1)S(1)}, bf16[4,128,128]{2,1,0:T(8,128)(2,1)S(1)}, u32[]{:S(2)}, u32[]{:S(2)}) %collective-permute-start.5) | collective-permute-done | bytes 131104 | tf_op jit(solution)/shard_map/ppermute | solution.py:280
  20.0 1.5 %collective-permute-done.6.refs_3_ = bf16[4,128,128]{2,1,0:T(8,128)(2,1)S(1)} collective-permute-done((bf16[4,128,128]{2,1,0:T(8,128)(2,1)S(1)}, bf16[4,128,128]{2,1,0:T(8,128)(2,1)S(1)}, u32[]{:S(2)}, u32[]{:S(2)}) %collective-permute-start.6) | collective-permute-done | bytes 131104 | tf_op jit(solution)/shard_map/ppermute | solution.py:280
  21.4 0.0 copy-start
  21.4 0.9 %copy-done = bf16[1,4,32,1024]{3,2,1,0:T(8,128)(2,1)S(1)} copy-done((bf16[1,4,32,1024]{3,2,1,0:T(8,128)(2,1)S(1)}, bf16[1,4,32,1024]{3,2,1,0:T(8,128)(2,1)}, u32[]{:S(2)}) %copy-start) | copy-done | bytes 262168
  22.4 0.0 copy-start.2
  22.4 0.7 %copy-done.2 = s32[16]{0:T(128)S(1)} copy-done((s32[16]{0:T(128)S(1)}, s32[16]{0:T(128)}, u32[]{:S(2)}) %copy-start.2) | copy-done | bytes 88
  23.0 0.0 copy-start.4
  23.0 0.7 %copy-done.4 = s32[16]{0:T(128)S(1)} copy-done((s32[16]{0:T(128)S(1)}, s32[16]{0:T(128)}, u32[]{:S(2)}) %copy-start.4) | copy-done | bytes 88
  23.7 0.0 copy-start.9
  23.7 0.5 %scale.1.refs_0_ = bf16[128,1024]{1,0:T(8,128)(2,1)S(1)} custom-call(s32[1,16]{1,0:T(1,128)S(1)} %bitcast.15, s32[1,16]{1,0:T(1,128)S(1)} %bitcast.16, bf16[128,1024]{1,0:T(8,128)(2,1)S(1)} %bitcast.13, bf16[4,128,128]{2,1,0:T(8,128)(2,1)S(1)} %pad_maximum_fusion.1.refs_0_, bf16[4,128,128]{2,1,0:T(8,128)(2,1)S(1)} %collective-permute-done.4.refs_1_, ...), custom_call_target="tpu_custom_call" | custom-call | flops 10000000 | bytes 1048576 | tf_op jit(solution)/shard_map/scale/pallas_call | solution.py:326
  24.2 0.0 copy-start.3
  24.2 0.0 copy-start.5
  24.2 0.0 copy-start.6
  24.3 0.0 copy-start.7
  24.3 0.0 copy-start.8
  24.3 0.1 collective-permute-start.7
  24.4 0.0 collective-permute-done
  24.4 0.0 copy-done.1
  24.4 0.3 copy-done.9
  24.6 0.1 pad_maximum_fusion.both_ref
  24.7 0.2 copy-done.3
  24.9 0.0 copy-done.5
  24.9 0.3 copy-done.6
  25.2 0.0 copy-done.7
  25.2 0.0 copy-done.8
  25.2 2.1 %forward.1 = (bf16[4,128,128]{2,1,0:T(8,128)(2,1)S(1)}, bf16[4,128,128]{2,1,0:T(8,128)(2,1)S(1)}, bf16[4,128,128]{2,1,0:T(8,128)(2,1)S(1)}, bf16[4,128,128]{2,1,0:T(8,128)(2,1)S(1)}, bf16[2,128,256]{2,1,0:T(8,128)(2,1)S(1)}) custom-call(s32[8,8]{1,0:T(8,128)S(1)} %copy-done.8, s32[16]{0:T(128)S(1)} %copy-done.3, s32[16]{0:T(128)S(1)} %copy-done.5, ...), custom_call_target="tpu_custom_call" | custom-call | flops 1000000000 | bytes 2097152 | tf_op jit(solution)/shard_map/forward/pallas_call | solution.py:292
  27.3 0.6 %collective-permute-start.8 = (bf16[4,128,128]{2,1,0:T(8,128)(2,1)S(1)}, bf16[4,128,128]{2,1,0:T(8,128)(2,1)S(1)}, u32[]{:S(2)}, u32[]{:S(2)}) collective-permute-start(bf16[4,128,128]{2,1,0:T(8,128)(2,1)S(1)} %get-tuple-element.15), channel_id=1, source_target_pairs={{0,2},{2,0},{4,6},{6,4},{8,10},{10,8},{12,14},{14,12},{16,18},{18,... | collective-permute-start | bytes 393224 | tf_op jit(solution)/shard_map/ppermute | solution.py:280
  27.9 0.5 %collective-permute-start.9 = (bf16[4,128,128]{2,1,0:T(8,128)(2,1)S(1)}, bf16[4,128,128]{2,1,0:T(8,128)(2,1)S(1)}, u32[]{:S(2)}, u32[]{:S(2)}) collective-permute-start(bf16[4,128,128]{2,1,0:T(8,128)(2,1)S(1)} %get-tuple-element.16), channel_id=1, source_target_pairs={{0,4},{2,6},{4,0},{6,2},{8,12},{10,14},{12,8},{14,10},{16,20},{18,... | collective-permute-start | bytes 393224 | tf_op jit(solution)/shard_map/ppermute | solution.py:280
  28.4 2.4 %collective-permute-start.10 = (bf16[4,128,128]{2,1,0:T(8,128)(2,1)S(1)}, bf16[4,128,128]{2,1,0:T(8,128)(2,1)S(1)}, u32[]{:S(2)}, u32[]{:S(2)}) collective-permute-start(bf16[4,128,128]{2,1,0:T(8,128)(2,1)S(1)} %get-tuple-element.17), channel_id=1, source_target_pairs={{0,6},{2,4},{4,2},{6,0},{8,14},{10,12},{12,10},{14,8},{16,22},{18,... | collective-permute-start | bytes 393224 | tf_op jit(solution)/shard_map/ppermute | solution.py:280
  30.9 2.9 %collective-permute-done.8.refs_1_ = bf16[4,128,128]{2,1,0:T(8,128)(2,1)S(1)} collective-permute-done((bf16[4,128,128]{2,1,0:T(8,128)(2,1)S(1)}, bf16[4,128,128]{2,1,0:T(8,128)(2,1)S(1)}, u32[]{:S(2)}, u32[]{:S(2)}) %collective-permute-start.8) | collective-permute-done | bytes 131104 | tf_op jit(solution)/shard_map/ppermute | solution.py:280
  33.7 0.3 collective-permute-done.9.refs_2_
  34.0 1.7 %collective-permute-done.10.refs_3_ = bf16[4,128,128]{2,1,0:T(8,128)(2,1)S(1)} collective-permute-done((bf16[4,128,128]{2,1,0:T(8,128)(2,1)S(1)}, bf16[4,128,128]{2,1,0:T(8,128)(2,1)S(1)}, u32[]{:S(2)}, u32[]{:S(2)}) %collective-permute-start.10) | collective-permute-done | bytes 131104 | tf_op jit(solution)/shard_map/ppermute | solution.py:280
  35.7 0.1 partial.1
  35.8 0.1 collective-permute-start.11
  35.9 1.4 %collective-permute-start.12 = (bf16[128,128]{1,0:T(8,128)(2,1)S(1)}, bf16[128,128]{1,0:T(8,128)(2,1)S(1)}, u32[]{:S(2)}, u32[]{:S(2)}) collective-permute-start(bf16[128,128]{1,0:T(8,128)(2,1)S(1)} %get-tuple-element.20), channel_id=1, source_target_pairs={{0,16},{2,18},{4,20},{6,22},{8,24},{10,26},{12,28},{14,30},{16,0},... | collective-permute-start | bytes 98312 | tf_op jit(solution)/shard_map/ppermute | solution.py:272
  37.3 2.7 %collective-permute-start.13 = (bf16[128,128]{1,0:T(8,128)(2,1)S(1)}, bf16[128,128]{1,0:T(8,128)(2,1)S(1)}, u32[]{:S(2)}, u32[]{:S(2)}) collective-permute-start(bf16[128,128]{1,0:T(8,128)(2,1)S(1)} %get-tuple-element.21), channel_id=1, source_target_pairs={{0,24},{2,26},{4,28},{6,30},{8,0},{10,2},{12,4},{14,6},{16,8},{18,... | collective-permute-start | bytes 98312 | tf_op jit(solution)/shard_map/ppermute | solution.py:272
  40.0 0.0 collective-permute-done.7.refs_1_
  40.0 1.6 %collective-permute-done.11.refs_3_ = bf16[128,128]{1,0:T(8,128)(2,1)S(1)} collective-permute-done((bf16[128,128]{1,0:T(8,128)(2,1)S(1)}, bf16[128,128]{1,0:T(8,128)(2,1)S(1)}, u32[]{:S(2)}, u32[]{:S(2)}) %collective-permute-start.11) | collective-permute-done | bytes 32800 | tf_op jit(solution)/shard_map/ppermute | solution.py:272
  41.6 0.0 collective-permute-done.12.refs_4_
  41.6 0.6 %collective-permute-done.13.refs_5_ = bf16[128,128]{1,0:T(8,128)(2,1)S(1)} collective-permute-done((bf16[128,128]{1,0:T(8,128)(2,1)S(1)}, bf16[128,128]{1,0:T(8,128)(2,1)S(1)}, u32[]{:S(2)}, u32[]{:S(2)}) %collective-permute-start.13) | collective-permute-done | bytes 32800 | tf_op jit(solution)/shard_map/ppermute | solution.py:272
  42.1 2.2 %backward.1 = (bf16[128,128]{1,0:T(8,128)(2,1)}, bf16[128,1024]{1,0:T(8,128)(2,1)}) custom-call(s32[8,8]{1,0:T(8,128)S(1)} %copy-done.8, bf16[2,128,256]{2,1,0:T(8,128)(2,1)S(1)} %get-tuple-element.13.up_ref, bf16[1024,128]{1,0:T(8,128)(2,1)S(1)} %bitcast.18, bf16[128,1024]{1,0:T(8,128)(2,1)S(1)} %scale.1.refs_0_, ...), custom_call_target="tpu_custom_call" | custom-call | flops 1000000000 | bytes 1048576 | tf_op jit(solution)/shard_map/backward/pallas_call | solution.py:340
Async XLA Ops:
  0.6 23.7 %copy-start.1 = (bf16[1,4,32,1024]{3,2,1,0:T(8,128)(2,1)S(1)}, bf16[1,4,32,1024]{3,2,1,0:T(8,128)(2,1)}, u32[]{:S(2)}) copy-start(bf16[1,4,32,1024]{3,2,1,0:T(8,128)(2,1)} %param.9) | copy-start | bytes 786436
  0.6 7.0 %collective-permute-start.3 = (bf16[128,128]{1,0:T(8,128)(2,1)}, bf16[128,128]{1,0:T(8,128)(2,1)S(1)}, u32[]{:S(2)}, u32[]{:S(2)}) collective-permute-start(bf16[128,128]{1,0:T(8,128)(2,1)} %bitcast.22), channel_id=1, source_target_pairs={{0,24},{2,26},{4,28},{6,30},{8,0},{10,2},{12,4},{14,6},{16,8},{18,... | collective-permute-start | bytes 98312 | tf_op jit(solution)/shard_map/ppermute | solution.py:272
  5.8 5.0 %collective-permute-start.2 = (bf16[128,128]{1,0:T(8,128)(2,1)}, bf16[128,128]{1,0:T(8,128)(2,1)S(1)}, u32[]{:S(2)}, u32[]{:S(2)}) collective-permute-start(bf16[128,128]{1,0:T(8,128)(2,1)} %bitcast.23), channel_id=1, source_target_pairs={{0,16},{2,18},{4,20},{6,22},{8,24},{10,26},{12,28},{14,30},{16,0},... | collective-permute-start | bytes 98312 | tf_op jit(solution)/shard_map/ppermute | solution.py:272
  5.8 5.9 %collective-permute-start.1 = (bf16[128,128]{1,0:T(8,128)(2,1)}, bf16[128,128]{1,0:T(8,128)(2,1)S(1)}, u32[]{:S(2)}, u32[]{:S(2)}) collective-permute-start(bf16[128,128]{1,0:T(8,128)(2,1)} %bitcast.24), channel_id=1, source_target_pairs={{0,8},{2,10},{4,12},{6,14},{8,16},{10,18},{12,20},{14,22},{16,24},... | collective-permute-start | bytes 98312 | tf_op jit(solution)/shard_map/ppermute | solution.py:272
  6.8 17.6 %collective-permute-start = (bf16[128,1024]{1,0:T(8,128)(2,1)}, bf16[128,1024]{1,0:T(8,128)(2,1)S(1)}, u32[]{:S(2)}, u32[]{:S(2)}) collective-permute-start(bf16[128,1024]{1,0:T(8,128)(2,1)} %bitcast.20), channel_id=1, source_target_pairs={{0,1},{1,0},{2,3},{3,2},{4,5},{5,4},{6,7},{7,6},{8,9},{9,8},{10,11... | collective-permute-start | bytes 786440 | tf_op jit(solution)/shard_map/ppermute | solution.py:21
  12.5 6.3 %collective-permute-start.4 = (bf16[4,128,128]{2,1,0:T(8,128)(2,1)S(1)}, bf16[4,128,128]{2,1,0:T(8,128)(2,1)S(1)}, u32[]{:S(2)}, u32[]{:S(2)}) collective-permute-start(bf16[4,128,128]{2,1,0:T(8,128)(2,1)S(1)} %pad_maximum_fusion.1.refs_0_), channel_id=1, source_target_pairs={{0,2},{2,0},{4,6},{6,4},{8,10},{10,8},{12,14},{14,12},{16,18},{18,... | collective-permute-start | bytes 393224 | tf_op jit(solution)/shard_map/ppermute | solution.py:280
  14.0 5.9 %collective-permute-start.5 = (bf16[4,128,128]{2,1,0:T(8,128)(2,1)S(1)}, bf16[4,128,128]{2,1,0:T(8,128)(2,1)S(1)}, u32[]{:S(2)}, u32[]{:S(2)}) collective-permute-start(bf16[4,128,128]{2,1,0:T(8,128)(2,1)S(1)} %pad_maximum_fusion.1.refs_0_), channel_id=1, source_target_pairs={{0,4},{2,6},{4,0},{6,2},{8,12},{10,14},{12,8},{14,10},{16,20},{18,... | collective-permute-start | bytes 393224 | tf_op jit(solution)/shard_map/ppermute | solution.py:280
  15.6 5.9 %collective-permute-start.6 = (bf16[4,128,128]{2,1,0:T(8,128)(2,1)S(1)}, bf16[4,128,128]{2,1,0:T(8,128)(2,1)S(1)}, u32[]{:S(2)}, u32[]{:S(2)}) collective-permute-start(bf16[4,128,128]{2,1,0:T(8,128)(2,1)S(1)} %pad_maximum_fusion.1.refs_0_), channel_id=1, source_target_pairs={{0,6},{2,4},{4,2},{6,0},{8,14},{10,12},{12,10},{14,8},{16,22},{18,... | collective-permute-start | bytes 393224 | tf_op jit(solution)/shard_map/ppermute | solution.py:280
  21.4 1.0 %copy-start = (bf16[1,4,32,1024]{3,2,1,0:T(8,128)(2,1)S(1)}, bf16[1,4,32,1024]{3,2,1,0:T(8,128)(2,1)}, u32[]{:S(2)}) copy-start(bf16[1,4,32,1024]{3,2,1,0:T(8,128)(2,1)} %param.9) | copy-start | bytes 786436
  22.4 0.7 %copy-start.2 = (s32[16]{0:T(128)S(1)}, s32[16]{0:T(128)}, u32[]{:S(2)}) copy-start(s32[16]{0:T(128)} %sizes.1) | copy-start | bytes 196
  23.0 0.7 %copy-start.4 = (s32[16]{0:T(128)S(1)}, s32[16]{0:T(128)}, u32[]{:S(2)}) copy-start(s32[16]{0:T(128)} %owner.1) | copy-start | bytes 196
  23.7 0.9 %copy-start.9 = (bf16[1,4,32,1024]{3,2,1,0:T(8,128)(2,1)S(1)}, bf16[1,4,32,1024]{3,2,1,0:T(8,128)(2,1)}, u32[]{:S(2)}) copy-start(bf16[1,4,32,1024]{3,2,1,0:T(8,128)(2,1)} %param.8) | copy-start | bytes 786436
  24.2 0.7 %copy-start.3 = (s32[16]{0:T(128)S(1)}, s32[16]{0:T(128)}, u32[]{:S(2)}) copy-start(s32[16]{0:T(128)} %sizes.1) | copy-start | bytes 196
  24.2 0.7 %copy-start.5 = (s32[16]{0:T(128)S(1)}, s32[16]{0:T(128)}, u32[]{:S(2)}) copy-start(s32[16]{0:T(128)} %owner.1) | copy-start | bytes 196
  24.2 1.0 %copy-start.6 = (bf16[8,128,128]{2,1,0:T(8,128)(2,1)S(1)}, bf16[8,128,128]{2,1,0:T(8,128)(2,1)}, u32[]{:S(2)}) copy-start(bf16[8,128,128]{2,1,0:T(8,128)(2,1)} %param.10) | copy-start | bytes 786436
  24.3 1.0 %copy-start.7 = (f32[64,9]{0,1:T(8,128)S(1)}, f32[64,9]{0,1:T(8,128)}, u32[]{:S(2)}) copy-start(f32[64,9]{0,1:T(8,128)} %param.11) | copy-start | bytes 6916
  24.3 1.0 %copy-start.8 = (s32[8,8]{1,0:T(8,128)S(1)}, s32[8,8]{1,0:T(8,128)}, u32[]{:S(2)}) copy-start(s32[8,8]{1,0:T(8,128)} %pattern.3) | copy-start | bytes 772
  24.3 15.7 %collective-permute-start.7 = (bf16[128,1024]{1,0:T(8,128)(2,1)S(1)}, bf16[128,1024]{1,0:T(8,128)(2,1)S(1)}, u32[]{:S(2)}, u32[]{:S(2)}) collective-permute-start(bf16[128,1024]{1,0:T(8,128)(2,1)S(1)} %scale.1.refs_0_), channel_id=1, source_target_pairs={{0,1},{1,0},{2,3},{3,2},{4,5},{5,4},{6,7},{7,6},{8,9},{9,8},{10,11... | collective-permute-start | bytes 786440 | tf_op jit(solution)/shard_map/ppermute | solution.py:21
  27.3 6.4 %collective-permute-start.8 = (bf16[4,128,128]{2,1,0:T(8,128)(2,1)S(1)}, bf16[4,128,128]{2,1,0:T(8,128)(2,1)S(1)}, u32[]{:S(2)}, u32[]{:S(2)}) collective-permute-start(bf16[4,128,128]{2,1,0:T(8,128)(2,1)S(1)} %get-tuple-element.15), channel_id=1, source_target_pairs={{0,2},{2,0},{4,6},{6,4},{8,10},{10,8},{12,14},{14,12},{16,18},{18,... | collective-permute-start | bytes 393224 | tf_op jit(solution)/shard_map/ppermute | solution.py:280
  27.9 6.1 %collective-permute-start.9 = (bf16[4,128,128]{2,1,0:T(8,128)(2,1)S(1)}, bf16[4,128,128]{2,1,0:T(8,128)(2,1)S(1)}, u32[]{:S(2)}, u32[]{:S(2)}) collective-permute-start(bf16[4,128,128]{2,1,0:T(8,128)(2,1)S(1)} %get-tuple-element.16), channel_id=1, source_target_pairs={{0,4},{2,6},{4,0},{6,2},{8,12},{10,14},{12,8},{14,10},{16,20},{18,... | collective-permute-start | bytes 393224 | tf_op jit(solution)/shard_map/ppermute | solution.py:280
  28.4 7.3 %collective-permute-start.10 = (bf16[4,128,128]{2,1,0:T(8,128)(2,1)S(1)}, bf16[4,128,128]{2,1,0:T(8,128)(2,1)S(1)}, u32[]{:S(2)}, u32[]{:S(2)}) collective-permute-start(bf16[4,128,128]{2,1,0:T(8,128)(2,1)S(1)} %get-tuple-element.17), channel_id=1, source_target_pairs={{0,6},{2,4},{4,2},{6,0},{8,14},{10,12},{12,10},{14,8},{16,22},{18,... | collective-permute-start | bytes 393224 | tf_op jit(solution)/shard_map/ppermute | solution.py:280
  35.8 5.8 %collective-permute-start.11 = (bf16[128,128]{1,0:T(8,128)(2,1)S(1)}, bf16[128,128]{1,0:T(8,128)(2,1)S(1)}, u32[]{:S(2)}, u32[]{:S(2)}) collective-permute-start(bf16[128,128]{1,0:T(8,128)(2,1)S(1)} %get-tuple-element.19), channel_id=1, source_target_pairs={{0,8},{2,10},{4,12},{6,14},{8,16},{10,18},{12,20},{14,22},{16,24},... | collective-permute-start | bytes 98312 | tf_op jit(solution)/shard_map/ppermute | solution.py:272
  35.9 5.7 %collective-permute-start.12 = (bf16[128,128]{1,0:T(8,128)(2,1)S(1)}, bf16[128,128]{1,0:T(8,128)(2,1)S(1)}, u32[]{:S(2)}, u32[]{:S(2)}) collective-permute-start(bf16[128,128]{1,0:T(8,128)(2,1)S(1)} %get-tuple-element.20), channel_id=1, source_target_pairs={{0,16},{2,18},{4,20},{6,22},{8,24},{10,26},{12,28},{14,30},{16,0},... | collective-permute-start | bytes 98312 | tf_op jit(solution)/shard_map/ppermute | solution.py:272
  37.3 4.9 %collective-permute-start.13 = (bf16[128,128]{1,0:T(8,128)(2,1)S(1)}, bf16[128,128]{1,0:T(8,128)(2,1)S(1)}, u32[]{:S(2)}, u32[]{:S(2)}) collective-permute-start(bf16[128,128]{1,0:T(8,128)(2,1)S(1)} %get-tuple-element.21), channel_id=1, source_target_pairs={{0,24},{2,26},{4,28},{6,30},{8,0},{10,2},{12,4},{14,6},{16,8},{18,... | collective-permute-start | bytes 98312 | tf_op jit(solution)/shard_map/ppermute | solution.py:272
